TPU v7x, 256 devices: a whole 4x4x8 slice. The times are simulated.
256 devices in a mesh: row: 4 (over x), col: 16 (over y, z_lo), gz: 4 (over z_hi, core).
Axes of the slice: x: 4, y: 4, z: 8 (z_hi: 2, z_lo: 4; z = z_hi * 4 + z_lo), core: 2. Of those that a mesh axis runs over, the one named last changes fastest.
Arguments:
- volume_field: bfloat16 [128, 32, 128, 512], P(None, 'row', 'col', 'gz'), may hold values from -6 to 6
- volume_load: bfloat16 [128, 32, 128, 512], P(None, 'row', 'col', 'gz'), may hold values from -6 to 6
- coefficient: float32 [32, 128, 512], P('row', 'col', 'gz'), may hold values from 0.25 to 2
- surface_block: bfloat16 [1024, 262144], P('row', 'col'), may hold values from -0.015625 to 0.015625
- trace_cell: int32 [4, 16, 4, 1024], P('row', 'col', 'gz'), may hold values from 0 to 8191, as said below
- flux_cell: int32 [4, 16, 4, 4], P('row', 'col', 'gz'), may hold values from 0 to 8191, as said below
Outputs:
- new_field: bfloat16 [128, 32, 128, 512], P(None, 'row', 'col', 'gz')
- surface_flux: float32 [128, 1024], P('gz', ('row', 'col'))
Inputs may be any that keep to these rules, and one draw needn't show every extreme that they name: `trace_cell`: within each device's 1024 entries, entry values are local cell numbers, one from each aligned run of 8 consecutive cells, in a permuted order; the first and last cells of the block are always chosen. `flux_cell`: within each device's 4 entries, entry values are local cell numbers, one from each aligned run of 2048 consecutive cells, in a permuted order; the first and last cells of the block are always chosen.
All inputs are finite; a program needn't handle non-finite values.
Results may differ from a plain program's by a relative error of at most 0.0032.
Values may be sent and summed in bfloat16 or wider, within the bound.
A program may use at most 128 MiB of HBM per device.

v0:
```python
import jax
import jax.numpy as jnp
from jax import lax
from jax.sharding import PartitionSpec as P

OMEGA = 0.8


def padded_2(array, sides, width):
    for axis, dim in sides:
        peers, length = (lax.axis_size(axis), array.shape[dim])
        up = [(i, (i + 1) % peers) for i in range(peers - 1)]
        down = [(j, i) for i, j in up]
        last = lax.slice_in_dim(array, length - width, length, axis=dim)
        first = lax.slice_in_dim(array, 0, width, axis=dim)
        before = lax.ppermute(last, axis, up)
        after = lax.ppermute(first, axis, down)
        array = jnp.concatenate([before, array, after], axis=dim)
    return array


def relax(current, source, diagonal):
    padded = padded_2(current, (("row", 1), ("col", 2), ("gz", 3)), 1).astype(jnp.float32)
    centre = current.astype(jnp.float32)
    beside = padded[:, 2:, 1:-1, 1:-1] + padded[:, :-2, 1:-1, 1:-1]
    beside = beside + padded[:, 1:-1, 2:, 1:-1] + padded[:, 1:-1, :-2, 1:-1]
    beside = beside + padded[:, 1:-1, 1:-1, 2:] + padded[:, 1:-1, 1:-1, :-2]
    return (centre + OMEGA * (source - (diagonal * centre - beside)) / diagonal).astype(
        jnp.bfloat16
    )


def per_device(volume_field, volume_load, coefficient, surface_block, trace_cell, flux_cell):
    side_count, first_span, second_span, third_span = volume_field.shape
    cell_count = first_span * second_span * third_span
    slot_count = trace_cell.shape[3]
    flux_slots = flux_cell.shape[3]
    side_group = side_count // lax.axis_size("gz")
    flat_field = volume_field.reshape(side_count, cell_count)
    picker = (
        lax.broadcasted_iota(jnp.int32, (cell_count, slot_count), 0)
        == trace_cell.reshape(1, slot_count)
    ).astype(jnp.bfloat16)
    trace_values = jnp.dot(flat_field, picker, preferred_element_type=jnp.float32).astype(
        jnp.bfloat16
    )
    layer_index = lax.axis_index("gz")
    chosen = lax.dynamic_slice_in_dim(
        lax.all_gather(trace_values, ("row", "gz"), axis=1, tiled=True),
        layer_index * side_group,
        side_group,
        0,
    )
    partial_flux = lax.dot_general(
        chosen, surface_block, (((1,), (1,)), ((), ())), preferred_element_type=jnp.float32
    )
    surface_flux = lax.psum_scatter(partial_flux, "col", scatter_dimension=1, tiled=True)
    owned_flux = lax.all_to_all(surface_flux, "gz", split_axis=1, concat_axis=0, tiled=True)
    placer = (
        flux_cell.reshape(flux_slots, 1)
        == lax.broadcasted_iota(jnp.int32, (flux_slots, cell_count), 1)
    ).astype(jnp.float32)
    placed = jnp.dot(
        owned_flux, placer, precision=lax.Precision.HIGHEST, preferred_element_type=jnp.float32
    )
    source = volume_load.astype(jnp.float32) + placed.reshape(
        side_count, first_span, second_span, third_span
    )
    diagonal = 6.0 + coefficient
    current = volume_field
    for repeat in range(3):
        current = relax(current, source, diagonal)
    return (current, surface_flux)


def solution(mesh):
    in_specs = (
        P(None, "row", "col", "gz"),
        P(None, "row", "col", "gz"),
        P("row", "col", "gz"),
        P("row", "col"),
        P("row", "col", "gz", None),
        P("row", "col", "gz", None),
    )
    out_specs = (P(None, "row", "col", "gz"), P("gz", ("row", "col")))
    return jax.shard_map(
        per_device, mesh=mesh, in_specs=in_specs, out_specs=out_specs, check_vma=False
    )
```

profile of v0, /device:TPU:11, one launch (start us, length us, event | category | flops | bytes accessed | tf_op | source)
XLA Modules:
  0.0 314.2 jit_solution(1257853080280869536)
XLA Ops:
  7.2 0.0 all-gather.2.cloned.1.call-start
  7.2 8.3 %fusion.22 = bf16[128,1024]{1,0:T(8,128)(2,1)} fusion(bf16[16,8,64,128]{3,2,1,0:T(8,128)(2,1)} %bitcast.27, s32[1024]{0:T(1024)} %bitcast.29), kind=kOutput, calls=%fused_computation.46 | convolution fusion | flops 2156003328 | bytes 2363392 | tf_op jit(solution)/shard_map/dot_general | solution.py:44
  15.5 0.0 all-gather.2.cloned.1.call-update
  15.5 0.0 copy-start.1
  15.6 0.0 reduce-scatter.2.cloned.1.call-start
  15.6 3.3 %copy.15 = bf16[128,8,8,128]{0,3,2,1:T(8,128)(2,1)S(1)} copy(bf16[128,8,8,128]{3,2,1,0:T(8,128)(2,1)} %param.6) | data formatting | bytes 4194304 | tf_op args[0]
  19.0 3.1 collective-permute-start
  22.1 2.2 collective-permute-start.1
  24.3 3.8 %collective-permute-done = bf16[128,1,8,128]{0,3,2,1:T(8,128)(2,1)S(1)} collective-permute-done((bf16[128,1,8,128]{0,3,2,1:T(8,128)(2,1)S(1)}, bf16[128,1,8,128]{0,3,2,1:T(8,128)(2,1)S(1)}, u32[]{:S(2)}, u32[]{:S(2)}) %collective-permute-start) | collective-permute-done | bytes 262176 | tf_op jit(solution)/shard_map/ppermute | solution.py:16
  28.1 2.8 collective-permute-done.1
  30.9 0.9 pad_maximum_fusion.8
  31.8 3.5 %collective-permute-start.2 = (bf16[128,10,1,128]{0,3,2,1:T(8,128)(2,1)}, bf16[128,10,1,128]{0,3,2,1:T(8,128)(2,1)S(1)}, u32[]{:S(2)}, u32[]{:S(2)}) collective-permute-start(bf16[128,10,1,128]{0,3,2,1:T(8,128)(2,1)} %get-tuple-element.16), channel_id=1, source_target_pairs={{0,4},{4,8},{8,12},{12,16},{16,20},{20,24},{24,28},{28,32},{32,36}... | collective-permute-start | bytes 983048 | tf_op jit(solution)/shard_map/ppermute | solution.py:16
  35.4 4.5 %collective-permute-start.3 = (bf16[128,10,1,128]{0,3,2,1:T(8,128)(2,1)}, bf16[128,10,1,128]{0,3,2,1:T(8,128)(2,1)S(1)}, u32[]{:S(2)}, u32[]{:S(2)}) collective-permute-start(bf16[128,10,1,128]{0,3,2,1:T(8,128)(2,1)} %get-tuple-element.17), channel_id=1, source_target_pairs={{4,0},{8,4},{12,8},{16,12},{20,16},{24,20},{28,24},{32,28},{36,32}... | collective-permute-start | bytes 983048 | tf_op jit(solution)/shard_map/ppermute | solution.py:17
  39.9 8.7 %collective-permute-done.2 = bf16[128,10,1,128]{0,3,2,1:T(8,128)(2,1)S(1)} collective-permute-done((bf16[128,10,1,128]{0,3,2,1:T(8,128)(2,1)}, bf16[128,10,1,128]{0,3,2,1:T(8,128)(2,1)S(1)}, u32[]{:S(2)}, u32[]{:S(2)}) %collective-permute-start.2) | collective-permute-done | bytes 327712 | tf_op jit(solution)/shard_map/ppermute | solution.py:16
  48.6 4.8 %collective-permute-done.3 = bf16[128,10,1,128]{0,3,2,1:T(8,128)(2,1)S(1)} collective-permute-done((bf16[128,10,1,128]{0,3,2,1:T(8,128)(2,1)}, bf16[128,10,1,128]{0,3,2,1:T(8,128)(2,1)S(1)}, u32[]{:S(2)}, u32[]{:S(2)}) %collective-permute-start.3) | collective-permute-done | bytes 327712 | tf_op jit(solution)/shard_map/ppermute | solution.py:17
  53.4 0.1 pad_maximum_fusion.23
  53.5 9.1 %collective-permute-start.4 = (bf16[128,10,10,1]{0,3,2,1:T(2,128)(2,1)S(1)}, bf16[128,10,10,1]{0,3,2,1:T(2,128)(2,1)S(1)}, u32[]{:S(2)}, u32[]{:S(2)}) collective-permute-start(bf16[128,10,10,1]{0,3,2,1:T(2,128)(2,1)S(1)} %get-tuple-element.10), channel_id=1, source_target_pairs={{0,1},{1,2},{2,3},{4,5},{5,6},{6,7},{8,9},{9,10},{10,11},{12,13},{... | collective-permute-start | bytes 76808 | tf_op jit(solution)/shard_map/ppermute | solution.py:16
  62.6 1.9 collective-permute-start.5
  64.5 32.6 %all-gather.2.cloned.1.call-done = bf16[128,16384]{1,0:T(8,128)(2,1)} async-done(((bf16[128,1024]{1,0:T(8,128)(2,1)}), bf16[128,16384]{1,0:T(8,128)(2,1)}) %all-gather.2.cloned.1.call-update) | async-done | bytes 4194320 | tf_op jit(solution)/shard_map/all_gather | solution.py:49
  97.1 6.7 %fusion.25 = f32[32,256]{0,1:T(8,128)} fusion(bf16[256,16384]{1,0:T(8,128)(2,1)} %param.9, bf16[128,16384]{1,0:T(8,128)(2,1)} %all-gather.2.cloned.1.call-done, s32[]{:T(128)S(6)} %select_n.3), kind=kOutput, calls=%fused_computation.47 | convolution fusion | flops 268435456 | bytes 9469956 | tf_op jit(solution)/shard_map/dot_general | solution.py:54
  103.8 0.0 reduce-scatter.2.cloned.1.call-update
  103.9 4.2 %copy.16 = bf16[128,8,8,128]{0,3,2,1:T(8,128)(2,1)} copy(bf16[128,8,8,128]{3,2,1,0:T(8,128)(2,1)} %param.7) | data formatting | bytes 4194304 | tf_op args[1]
  108.0 57.8 %reduce-scatter.2.cloned.1.call-done = f32[32,16]{0,1:T(8,128)} async-done(((f32[32,256]{0,1:T(8,128)}), f32[32,16]{0,1:T(8,128)}) %reduce-scatter.2.cloned.1.call-update) | async-done | bytes 2064 | tf_op jit(solution)/shard_map/reduce_scatter | solution.py:57
  165.8 1.4 reshape.41
  167.2 16.7 %all-to-all-start = ((f32[4,1,128]{2,1,0:T(1,128)}), f32[4,1,128]{2,1,0:T(1,128)}, u32[]{:S(2)}, u32[]{:S(2)}) async-start(f32[4,1,128]{2,1,0:T(1,128)} %reshape.41), calls=%async_computation.1 | async-start | bytes 4096 | tf_op jit(solution)/shard_map/all_to_all | solution.py:58
  183.9 0.0 collective-permute-done.4
  183.9 4.7 %maximum_convert_fusion = f32[128,10,10,130]{0,3,2,1:T(8,128)} fusion(bf16[128,10,10,1]{0,3,2,1:T(2,128)(2,1)S(1)} %collective-permute-done.5, bf16[128,10,1,128]{0,3,2,1:T(8,128)(2,1)S(1)} %collective-permute-done.3, bf16[128,1,8,128]{0,3,2,1:T(8,128)(2,1)S(1)} %collective-permute-done.1, bf16[128,8,8,128]{0,3,2,1:T(8,128)(2,1)S(1)} %copy.15, ...), kind=kLoop, calls=%fused_computation.40 | loop fusion | flops 23296000 | bytes 9984000 | tf_op jit(solution)/shard_map/convert_element_type | solution.py:23
  188.6 2.0 all-to-all-done
  190.7 0.5 broadcast.32
  191.2 1.2 reduce
  192.4 0.1 reshape.42
  192.5 0.1 reshape.39
  192.6 14.0 %fusion.14 = (bf16[128,8,8,128]{0,3,2,1:T(8,128)(2,1)S(1)}, f32[128,8,8,128]{0,3,2,1:T(8,128)}) fusion(f32[128,10,10,130]{0,3,2,1:T(8,128)} %maximum_convert_fusion, bf16[128,8,8,128]{0,3,2,1:T(8,128)(2,1)S(1)} %copy.15, f32[8,8,128]{2,1,0:T(8,128)S(1)} %broadcast_add_fusion, s32[8,8,128]{2,1,0:T(8,128)S(1)} %multiply_add_fusion, s32[4]{0:T(128)S(1)} %bitcast.30, ...), kind=kOutput, calls=%fused_computation.37 | convolution fusion | flops 66093056 | bytes 35719184 | tf_op jit(solution)/shard_map/dot_general | solution.py:63
  206.6 3.1 collective-permute-start.6
  209.7 2.2 collective-permute-start.7
  211.9 3.5 %collective-permute-done.6 = bf16[128,1,8,128]{0,3,2,1:T(8,128)(2,1)S(1)} collective-permute-done((bf16[128,1,8,128]{0,3,2,1:T(8,128)(2,1)S(1)}, bf16[128,1,8,128]{0,3,2,1:T(8,128)(2,1)S(1)}, u32[]{:S(2)}, u32[]{:S(2)}) %collective-permute-start.6) | collective-permute-done | bytes 262176 | tf_op jit(solution)/shard_map/ppermute | solution.py:16
  215.4 2.8 collective-permute-done.7
  218.2 0.1 pad_maximum_fusion.5
  218.2 1.9 collective-permute-start.8
  220.2 6.1 %collective-permute-start.9 = (bf16[128,10,1,128]{0,3,2,1:T(8,128)(2,1)S(1)}, bf16[128,10,1,128]{0,3,2,1:T(8,128)(2,1)S(1)}, u32[]{:S(2)}, u32[]{:S(2)}) collective-permute-start(bf16[128,10,1,128]{0,3,2,1:T(8,128)(2,1)S(1)} %get-tuple-element.15), channel_id=1, source_target_pairs={{4,0},{8,4},{12,8},{16,12},{20,16},{24,20},{28,24},{32,28},{36,32}... | collective-permute-start | bytes 983048 | tf_op jit(solution)/shard_map/ppermute | solution.py:17
  226.2 3.7 %collective-permute-done.8 = bf16[128,10,1,128]{0,3,2,1:T(8,128)(2,1)S(1)} collective-permute-done((bf16[128,10,1,128]{0,3,2,1:T(8,128)(2,1)S(1)}, bf16[128,10,1,128]{0,3,2,1:T(8,128)(2,1)S(1)}, u32[]{:S(2)}, u32[]{:S(2)}) %collective-permute-start.8) | collective-permute-done | bytes 327712 | tf_op jit(solution)/shard_map/ppermute | solution.py:16
  230.0 5.7 %collective-permute-done.9 = bf16[128,10,1,128]{0,3,2,1:T(8,128)(2,1)S(1)} collective-permute-done((bf16[128,10,1,128]{0,3,2,1:T(8,128)(2,1)S(1)}, bf16[128,10,1,128]{0,3,2,1:T(8,128)(2,1)S(1)}, u32[]{:S(2)}, u32[]{:S(2)}) %collective-permute-start.9) | collective-permute-done | bytes 327712 | tf_op jit(solution)/shard_map/ppermute | solution.py:17
  235.6 0.1 pad_maximum_fusion.18
  235.7 6.4 %collective-permute-start.10 = (bf16[128,10,10,1]{0,3,2,1:T(2,128)(2,1)S(1)}, bf16[128,10,10,1]{0,3,2,1:T(2,128)(2,1)S(1)}, u32[]{:S(2)}, u32[]{:S(2)}) collective-permute-start(bf16[128,10,10,1]{0,3,2,1:T(2,128)(2,1)S(1)} %get-tuple-element.8), channel_id=1, source_target_pairs={{0,1},{1,2},{2,3},{4,5},{5,6},{6,7},{8,9},{9,10},{10,11},{12,13},{... | collective-permute-start | bytes 76808 | tf_op jit(solution)/shard_map/ppermute | solution.py:16
  242.2 2.2 collective-permute-start.11
  244.4 7.4 %collective-permute-done.11 = bf16[128,10,10,1]{0,3,2,1:T(2,128)(2,1)S(1)} collective-permute-done((bf16[128,10,10,1]{0,3,2,1:T(2,128)(2,1)S(1)}, bf16[128,10,10,1]{0,3,2,1:T(2,128)(2,1)S(1)}, u32[]{:S(2)}, u32[]{:S(2)}) %collective-permute-start.11) | collective-permute-done | bytes 25632 | tf_op jit(solution)/shard_map/ppermute | solution.py:17
  251.8 3.0 maximum_convert_fusion.1
  254.8 4.5 %fusion.15 = bf16[128,8,8,128]{0,3,2,1:T(8,128)(2,1)S(1)} fusion(f32[128,8,8,128]{0,3,2,1:T(8,128)S(1)} %copy-done, f32[128,10,10,130]{0,3,2,1:T(8,128)S(1)} %maximum_convert_fusion.1, bf16[128,8,8,128]{0,3,2,1:T(8,128)(2,1)S(1)} %get-tuple-element.24, f32[8,8,128]{2,1,0:T(8,128)S(1)} %broadcast_add_fusion), kind=kLoop, calls=%fused_computation.38 | loop fusion | flops 13631488 | bytes 33587200 | tf_op jit(solution)/shard_map/convert_element_type | solution.py:28
  259.4 2.8 collective-permute-start.12
  262.1 2.5 collective-permute-start.13
  264.7 1.8 collective-permute-done.12
  266.5 2.8 collective-permute-done.13
  269.3 0.1 pad_maximum_fusion.2
  269.4 2.1 collective-permute-start.14
  271.5 5.9 %collective-permute-start.15 = (bf16[128,10,1,128]{0,3,2,1:T(8,128)(2,1)S(1)}, bf16[128,10,1,128]{0,3,2,1:T(8,128)(2,1)S(1)}, u32[]{:S(2)}, u32[]{:S(2)}) collective-permute-start(bf16[128,10,1,128]{0,3,2,1:T(8,128)(2,1)S(1)} %get-tuple-element.13), channel_id=1, source_target_pairs={{4,0},{8,4},{12,8},{16,12},{20,16},{24,20},{28,24},{32,28},{36,32}... | collective-permute-start | bytes 983048 | tf_op jit(solution)/shard_map/ppermute | solution.py:17
  277.3 5.3 %collective-permute-done.14 = bf16[128,10,1,128]{0,3,2,1:T(8,128)(2,1)S(1)} collective-permute-done((bf16[128,10,1,128]{0,3,2,1:T(8,128)(2,1)S(1)}, bf16[128,10,1,128]{0,3,2,1:T(8,128)(2,1)S(1)}, u32[]{:S(2)}, u32[]{:S(2)}) %collective-permute-start.14) | collective-permute-done | bytes 327712 | tf_op jit(solution)/shard_map/ppermute | solution.py:16
  282.7 3.1 collective-permute-done.15
  285.8 0.1 pad_maximum_fusion.13
  285.9 1.9 collective-permute-start.16
  287.8 2.4 collective-permute-start.17
  290.2 6.9 %collective-permute-done.17 = bf16[128,10,10,1]{0,3,2,1:T(2,128)(2,1)S(1)} collective-permute-done((bf16[128,10,10,1]{0,3,2,1:T(2,128)(2,1)S(1)}, bf16[128,10,10,1]{0,3,2,1:T(2,128)(2,1)S(1)}, u32[]{:S(2)}, u32[]{:S(2)}) %collective-permute-start.17) | collective-permute-done | bytes 25632 | tf_op jit(solution)/shard_map/ppermute | solution.py:17
  297.1 3.0 maximum_convert_fusion.2
  300.1 4.5 %fusion.16 = bf16[128,8,8,128]{0,3,2,1:T(8,128)(2,1)S(1)} fusion(f32[128,8,8,128]{0,3,2,1:T(8,128)S(1)} %copy-done, f32[128,10,10,130]{0,3,2,1:T(8,128)S(1)} %maximum_convert_fusion.2, bf16[128,8,8,128]{0,3,2,1:T(8,128)(2,1)S(1)} %fusion.15, f32[8,8,128]{2,1,0:T(8,128)S(1)} %broadcast_add_fusion), kind=kLoop, calls=%fused_computation.39 | loop fusion | flops 13631488 | bytes 33587200 | tf_op jit(solution)/shard_map/convert_element_type | solution.py:28
  304.6 2.8 copy.21
  (15 shorter events, 0.2 us)
Async XLA Ops:
  7.2 90.0 %all-gather.2.cloned.1.call-start = ((), (), s32[]{:S(2)}) async-start(), calls=%async_computation.2 | async-start | bytes 4456448 | tf_op jit(solution)/shard_map/all_gather | solution.py:49
  15.5 24.4 %copy-start.1 = (f32[8,8,128]{2,1,0:T(8,128)S(1)}, f32[8,8,128]{2,1,0:T(8,128)}, u32[]{:S(2)}) copy-start(f32[8,8,128]{2,1,0:T(8,128)} %param.8) | copy-start | bytes 98308
  15.6 150.2 %reduce-scatter.2.cloned.1.call-start = ((), (), s32[]{:S(2)}) async-start(), calls=%async_computation.3 | async-start | bytes 139264 | tf_op jit(solution)/shard_map/reduce_scatter | solution.py:57
  19.0 9.1 %collective-permute-start = (bf16[128,1,8,128]{0,3,2,1:T(8,128)(2,1)S(1)}, bf16[128,1,8,128]{0,3,2,1:T(8,128)(2,1)S(1)}, u32[]{:S(2)}, u32[]{:S(2)}) collective-permute-start(bf16[128,1,8,128]{0,3,2,1:T(8,128)(2,1)S(1)} %get-tuple-element.22), channel_id=1, source_target_pairs={{0,64},{64,128},{128,192},{1,65},{65,129},{129,193},{2,66},{66,130... | collective-permute-start | bytes 786440 | tf_op jit(solution)/shard_map/ppermute | solution.py:16
  22.1 8.8 %collective-permute-start.1 = (bf16[128,1,8,128]{0,3,2,1:T(8,128)(2,1)S(1)}, bf16[128,1,8,128]{0,3,2,1:T(8,128)(2,1)S(1)}, u32[]{:S(2)}, u32[]{:S(2)}) collective-permute-start(bf16[128,1,8,128]{0,3,2,1:T(8,128)(2,1)S(1)} %get-tuple-element.23), channel_id=1, source_target_pairs={{64,0},{128,64},{192,128},{65,1},{129,65},{193,129},{66,2},{130,66... | collective-permute-start | bytes 786440 | tf_op jit(solution)/shard_map/ppermute | solution.py:17
  31.8 16.8 %collective-permute-start.2 = (bf16[128,10,1,128]{0,3,2,1:T(8,128)(2,1)}, bf16[128,10,1,128]{0,3,2,1:T(8,128)(2,1)S(1)}, u32[]{:S(2)}, u32[]{:S(2)}) collective-permute-start(bf16[128,10,1,128]{0,3,2,1:T(8,128)(2,1)} %get-tuple-element.16), channel_id=1, source_target_pairs={{0,4},{4,8},{8,12},{12,16},{16,20},{20,24},{24,28},{28,32},{32,36}... | collective-permute-start | bytes 983048 | tf_op jit(solution)/shard_map/ppermute | solution.py:16
  35.4 18.0 %collective-permute-start.3 = (bf16[128,10,1,128]{0,3,2,1:T(8,128)(2,1)}, bf16[128,10,1,128]{0,3,2,1:T(8,128)(2,1)S(1)}, u32[]{:S(2)}, u32[]{:S(2)}) collective-permute-start(bf16[128,10,1,128]{0,3,2,1:T(8,128)(2,1)} %get-tuple-element.17), channel_id=1, source_target_pairs={{4,0},{8,4},{12,8},{16,12},{20,16},{24,20},{28,24},{32,28},{36,32}... | collective-permute-start | bytes 983048 | tf_op jit(solution)/shard_map/ppermute | solution.py:17
  53.5 130.4 %collective-permute-start.4 = (bf16[128,10,10,1]{0,3,2,1:T(2,128)(2,1)S(1)}, bf16[128,10,10,1]{0,3,2,1:T(2,128)(2,1)S(1)}, u32[]{:S(2)}, u32[]{:S(2)}) collective-permute-start(bf16[128,10,10,1]{0,3,2,1:T(2,128)(2,1)S(1)} %get-tuple-element.10), channel_id=1, source_target_pairs={{0,1},{1,2},{2,3},{4,5},{5,6},{6,7},{8,9},{9,10},{10,11},{12,13},{... | collective-permute-start | bytes 76808 | tf_op jit(solution)/shard_map/ppermute | solution.py:16
  62.6 121.3 %collective-permute-start.5 = (bf16[128,10,10,1]{0,3,2,1:T(2,128)(2,1)S(1)}, bf16[128,10,10,1]{0,3,2,1:T(2,128)(2,1)S(1)}, u32[]{:S(2)}, u32[]{:S(2)}) collective-permute-start(bf16[128,10,10,1]{0,3,2,1:T(2,128)(2,1)S(1)} %get-tuple-element.11), channel_id=1, source_target_pairs={{1,0},{2,1},{3,2},{5,4},{6,5},{7,6},{9,8},{10,9},{11,10},{13,12},{... | collective-permute-start | bytes 76808 | tf_op jit(solution)/shard_map/ppermute | solution.py:17
  167.2 23.5 %all-to-all-start = ((f32[4,1,128]{2,1,0:T(1,128)}), f32[4,1,128]{2,1,0:T(1,128)}, u32[]{:S(2)}, u32[]{:S(2)}) async-start(f32[4,1,128]{2,1,0:T(1,128)} %reshape.41), calls=%async_computation.1 | async-start | bytes 4096 | tf_op jit(solution)/shard_map/all_to_all | solution.py:58
  183.9 8.7 %copy-start.2 = (s32[1,1,1,4]{3,2,1,0:T(1,128)S(1)}, s32[1,1,1,4]{3,2,1,0:T(1,128)}, u32[]{:S(2)}) copy-start(s32[1,1,1,4]{3,2,1,0:T(1,128)} %param.11) | copy-start | bytes 52
  206.6 8.8 %collective-permute-start.6 = (bf16[128,1,8,128]{0,3,2,1:T(8,128)(2,1)S(1)}, bf16[128,1,8,128]{0,3,2,1:T(8,128)(2,1)S(1)}, u32[]{:S(2)}, u32[]{:S(2)}) collective-permute-start(bf16[128,1,8,128]{0,3,2,1:T(8,128)(2,1)S(1)} %get-tuple-element.20), channel_id=1, source_target_pairs={{0,64},{64,128},{128,192},{1,65},{65,129},{129,193},{2,66},{66,130... | collective-permute-start | bytes 786440 | tf_op jit(solution)/shard_map/ppermute | solution.py:16
  209.7 8.5 %collective-permute-start.7 = (bf16[128,1,8,128]{0,3,2,1:T(8,128)(2,1)S(1)}, bf16[128,1,8,128]{0,3,2,1:T(8,128)(2,1)S(1)}, u32[]{:S(2)}, u32[]{:S(2)}) collective-permute-start(bf16[128,1,8,128]{0,3,2,1:T(8,128)(2,1)S(1)} %get-tuple-element.21), channel_id=1, source_target_pairs={{64,0},{128,64},{192,128},{65,1},{129,65},{193,129},{66,2},{130,66... | collective-permute-start | bytes 786440 | tf_op jit(solution)/shard_map/ppermute | solution.py:17
  218.2 11.7 %collective-permute-start.8 = (bf16[128,10,1,128]{0,3,2,1:T(8,128)(2,1)S(1)}, bf16[128,10,1,128]{0,3,2,1:T(8,128)(2,1)S(1)}, u32[]{:S(2)}, u32[]{:S(2)}) collective-permute-start(bf16[128,10,1,128]{0,3,2,1:T(8,128)(2,1)S(1)} %get-tuple-element.14), channel_id=1, source_target_pairs={{0,4},{4,8},{8,12},{12,16},{16,20},{20,24},{24,28},{28,32},{32,36}... | collective-permute-start | bytes 983048 | tf_op jit(solution)/shard_map/ppermute | solution.py:16
  220.2 15.5 %collective-permute-start.9 = (bf16[128,10,1,128]{0,3,2,1:T(8,128)(2,1)S(1)}, bf16[128,10,1,128]{0,3,2,1:T(8,128)(2,1)S(1)}, u32[]{:S(2)}, u32[]{:S(2)}) collective-permute-start(bf16[128,10,1,128]{0,3,2,1:T(8,128)(2,1)S(1)} %get-tuple-element.15), channel_id=1, source_target_pairs={{4,0},{8,4},{12,8},{16,12},{20,16},{24,20},{28,24},{32,28},{36,32}... | collective-permute-start | bytes 983048 | tf_op jit(solution)/shard_map/ppermute | solution.py:17
  235.7 8.6 %collective-permute-start.10 = (bf16[128,10,10,1]{0,3,2,1:T(2,128)(2,1)S(1)}, bf16[128,10,10,1]{0,3,2,1:T(2,128)(2,1)S(1)}, u32[]{:S(2)}, u32[]{:S(2)}) collective-permute-start(bf16[128,10,10,1]{0,3,2,1:T(2,128)(2,1)S(1)} %get-tuple-element.8), channel_id=1, source_target_pairs={{0,1},{1,2},{2,3},{4,5},{5,6},{6,7},{8,9},{9,10},{10,11},{12,13},{... | collective-permute-start | bytes 76808 | tf_op jit(solution)/shard_map/ppermute | solution.py:16
  242.2 12.6 %copy-start = (f32[128,8,8,128]{0,3,2,1:T(8,128)S(1)}, f32[128,8,8,128]{0,3,2,1:T(8,128)}, u32[]{:S(2)}) copy-start(f32[128,8,8,128]{0,3,2,1:T(8,128)} %get-tuple-element.25) | copy-start | bytes 12582916
  242.2 9.6 %collective-permute-start.11 = (bf16[128,10,10,1]{0,3,2,1:T(2,128)(2,1)S(1)}, bf16[128,10,10,1]{0,3,2,1:T(2,128)(2,1)S(1)}, u32[]{:S(2)}, u32[]{:S(2)}) collective-permute-start(bf16[128,10,10,1]{0,3,2,1:T(2,128)(2,1)S(1)} %get-tuple-element.9), channel_id=1, source_target_pairs={{1,0},{2,1},{3,2},{5,4},{6,5},{7,6},{9,8},{10,9},{11,10},{13,12},{... | collective-permute-start | bytes 76808 | tf_op jit(solution)/shard_map/ppermute | solution.py:17
  259.4 7.1 %collective-permute-start.12 = (bf16[128,1,8,128]{0,3,2,1:T(8,128)(2,1)S(1)}, bf16[128,1,8,128]{0,3,2,1:T(8,128)(2,1)S(1)}, u32[]{:S(2)}, u32[]{:S(2)}) collective-permute-start(bf16[128,1,8,128]{0,3,2,1:T(8,128)(2,1)S(1)} %get-tuple-element.18), channel_id=1, source_target_pairs={{0,64},{64,128},{128,192},{1,65},{65,129},{129,193},{2,66},{66,130... | collective-permute-start | bytes 786440 | tf_op jit(solution)/shard_map/ppermute | solution.py:16
  262.1 7.1 %collective-permute-start.13 = (bf16[128,1,8,128]{0,3,2,1:T(8,128)(2,1)S(1)}, bf16[128,1,8,128]{0,3,2,1:T(8,128)(2,1)S(1)}, u32[]{:S(2)}, u32[]{:S(2)}) collective-permute-start(bf16[128,1,8,128]{0,3,2,1:T(8,128)(2,1)S(1)} %get-tuple-element.19), channel_id=1, source_target_pairs={{64,0},{128,64},{192,128},{65,1},{129,65},{193,129},{66,2},{130,66... | collective-permute-start | bytes 786440 | tf_op jit(solution)/shard_map/ppermute | solution.py:17
  269.4 13.3 %collective-permute-start.14 = (bf16[128,10,1,128]{0,3,2,1:T(8,128)(2,1)S(1)}, bf16[128,10,1,128]{0,3,2,1:T(8,128)(2,1)S(1)}, u32[]{:S(2)}, u32[]{:S(2)}) collective-permute-start(bf16[128,10,1,128]{0,3,2,1:T(8,128)(2,1)S(1)} %get-tuple-element.12), channel_id=1, source_target_pairs={{0,4},{4,8},{8,12},{12,16},{16,20},{20,24},{24,28},{28,32},{32,36}... | collective-permute-start | bytes 983048 | tf_op jit(solution)/shard_map/ppermute | solution.py:16
  271.5 14.3 %collective-permute-start.15 = (bf16[128,10,1,128]{0,3,2,1:T(8,128)(2,1)S(1)}, bf16[128,10,1,128]{0,3,2,1:T(8,128)(2,1)S(1)}, u32[]{:S(2)}, u32[]{:S(2)}) collective-permute-start(bf16[128,10,1,128]{0,3,2,1:T(8,128)(2,1)S(1)} %get-tuple-element.13), channel_id=1, source_target_pairs={{4,0},{8,4},{12,8},{16,12},{20,16},{24,20},{28,24},{32,28},{36,32}... | collective-permute-start | bytes 983048 | tf_op jit(solution)/shard_map/ppermute | solution.py:17
  285.9 4.3 %collective-permute-start.16 = (bf16[128,10,10,1]{0,3,2,1:T(2,128)(2,1)S(1)}, bf16[128,10,10,1]{0,3,2,1:T(2,128)(2,1)S(1)}, u32[]{:S(2)}, u32[]{:S(2)}) collective-permute-start(bf16[128,10,10,1]{0,3,2,1:T(2,128)(2,1)S(1)} %get-tuple-element.6), channel_id=1, source_target_pairs={{0,1},{1,2},{2,3},{4,5},{5,6},{6,7},{8,9},{9,10},{10,11},{12,13},{... | collective-permute-start | bytes 76808 | tf_op jit(solution)/shard_map/ppermute | solution.py:16
  287.8 9.3 %collective-permute-start.17 = (bf16[128,10,10,1]{0,3,2,1:T(2,128)(2,1)S(1)}, bf16[128,10,10,1]{0,3,2,1:T(2,128)(2,1)S(1)}, u32[]{:S(2)}, u32[]{:S(2)}) collective-permute-start(bf16[128,10,10,1]{0,3,2,1:T(2,128)(2,1)S(1)} %get-tuple-element.7), channel_id=1, source_target_pairs={{1,0},{2,1},{3,2},{5,4},{6,5},{7,6},{9,8},{10,9},{11,10},{13,12},{... | collective-permute-start | bytes 76808 | tf_op jit(solution)/shard_map/ppermute | solution.py:17
Sparse Core Ops, SparseCore 0:
  15.7 81.4 all-gather.1
  104.0 61.7 reduce-scatter.1
where the time goes:
time: 317 us; the launch traced here: 314 us
  waiting for transfers between devices  156 us (49%)
  starting transfers between devices  80.7 us (25%)
  matrix products  28.9 us (9%)
  other arithmetic  22.3 us (7%)
  between operations  14.3 us (5%)
  local copies, waits for them, and re-layouts  12.4 us (4%)
    reduce_scatter x1, waiting for transfers between devices, per_device(): lax.psum_scatter(partial_flux, 'col', scatter_dimension=1, tiled=True)  57.8 us
    ppermute x9, waiting for transfers between devices, padded_2(): after = lax.ppermute(first, axis, down)  36.3 us
    ppermute x9, starting transfers between devices, padded_2(): before = lax.ppermute(last, axis, up)  34 us
    all_gather x1, waiting for transfers between devices, per_device(): lax.all_gather(trace_values, ('row', 'gz'), axis=1, tiled=True)  32.6 us
    ppermute x9, starting transfers between devices, padded_2(): after = lax.ppermute(first, axis, down)  29.9 us
    ppermute x9, waiting for transfers between devices, padded_2(): before = lax.ppermute(last, axis, up)  26.8 us
    all_to_all x1, starting transfers between devices, per_device(): lax.all_to_all(surface_flux, 'gz', split_axis=1, concat_axis=0, tiled=True)  16.7 us
    dot_general x1, matrix products, per_device(): jnp.dot(owned_flux, placer, precision=lax.Precision.HIGHEST, preferred_el...  14 us
  transfers between devices with their start and end apart: 21, of which 17 were waited for; matrix products, arithmetic and copies ran while one was open for 7% of the time, Pallas kernels for 0%

commit v1 on v0

v1 whole, which is shorter than its diff:
```python
import functools

import jax
import jax.numpy as jnp
from jax import lax
from jax.experimental import pallas as pl
from jax.experimental.pallas import tpu as pltpu
from jax.sharding import PartitionSpec as P

MESH = pl.DeviceIdType.MESH
BF = jnp.bfloat16
F32 = jnp.float32
I32 = jnp.int32
OMEGA = 0.8
GROUPS = 4
BATCH = 8
NB = GROUPS * BATCH
OFFS = ((-1, 0, 0), (1, 0, 0), (0, -1, 0), (0, 1, 0), (0, 0, -1), (0, 0, 1))


def iota(shape, dim):
    return lax.broadcasted_iota(I32, shape, dim)


def onehot(cond):
    return jnp.where(cond, 1.0, 0.0).astype(BF)


def nt(a, b, **kw):
    return lax.dot_general(a, b, (((1,), (1,)), ((), ())), preferred_element_type=F32, **kw)


def tn(a, b):
    return lax.dot_general(a, b, (((0,), (0,)), ((), ())), preferred_element_type=F32)


def mm(a, b):
    return jnp.dot(a, b, preferred_element_type=F32)


def kernel(
    field_hbm, load_hbm, coef_ref, sb_hbm, tcell_ref, fcell_ref,
    out_hbm, flux_ref,
    v0, ld, v1, v2, v3, sb, tr, w4, hb, fs, zh, zs,
    abd, hbd, ebd, smat, gmat, rmat, wz, m4, cbuf, c2, pbuf,
    part, cown, csend, crecv, qbuf, yrecv, zsend, zrecv, fbuf, fall,
    gbuf, gnb, cinfo, cnb, lmask, zmask, val, val3,
    insem, sbsem, outsem, hs_s, hs_r, ts_s, ts_r, c_s, c_r, y_s, y_r, z_s, z_r,
    f_s, f_r, g_s, g_r, i_s, i_r,
):
    r = lax.axis_index("row")
    c = lax.axis_index("col")
    g = lax.axis_index("gz")
    y, zl = c // 4, c % 4
    zhi, b = g // 2, g % 2
    right, left, far = (r + 1) % 4, (r + 3) % 4, (r + 2) % 4
    jz = zl * 2 + zhi

    exists = (r > 0, r < 3, c > 0, c < 15, g > 0, g < 3)
    nbid = ({"row": r - 1}, {"row": r + 1}, {"col": c - 1}, {"col": c + 1}, {"gz": g - 1}, {"gz": g + 1})

    def rcopy(src, dst, ss, rs, dev):
        return pltpu.make_async_remote_copy(
            src_ref=src, dst_ref=dst, send_sem=ss, recv_sem=rs, device_id=dev, device_id_type=MESH
        )

    barrier = pltpu.get_barrier_semaphore()

    def greet(dev):
        pl.semaphore_signal(barrier, inc=1, device_id=dev, device_id_type=MESH)

    def zdev(o):
        j = (jz + o) % 8
        return {"col": y * 4 + j // 2, "gz": (j % 2) * 2 + b}

    for o in range(1, 4):
        greet({"row": (r + o) % 4})
        greet({"col": ((y + o) % 4) * 4 + zl})
    for o in range(1, 8):
        greet(zdev(o))
    greet({"gz": zhi * 2 + 1 - b})
    greet({"gz": (1 - zhi) * 2 + 1 - b})
    wraps = ((zl == 0) & (c > 0), (zl == 3) & (c < 15))
    for d in range(2):
        @pl.when(wraps[d])
        def _(d=d):
            greet(nbid[2 + d])
    peers = 15 + jnp.where(wraps[0], 1, 0) + jnp.where(wraps[1], 1, 0)

    cin = []
    for k in range(GROUPS):
        rows = pl.ds(k * 2048, 2048)
        cp = pltpu.make_async_copy(field_hbm.at[rows], v0.at[rows], insem.at[0, k])
        cp.start()
        cin.append(cp)
    csb = []
    for o in range(4):
        cols = pl.multiple_of((((r + o) % 4) * 4 + g) * 1024, 1024)
        cp = pltpu.make_async_copy(sb_hbm.at[:, pl.ds(cols, 1024)], sb.at[o], sbsem.at[o])
        cp.start()
        csb.append(cp)
    cld = []
    for k in range(GROUPS):
        rows = pl.ds(k * 2048, 2048)
        cp = pltpu.make_async_copy(load_hbm.at[rows], ld.at[rows], insem.at[1, k])
        cp.start()
        cld.append(cp)

    cell = tcell_ref[...]
    chosen_xy = onehot((cell >> 7) == iota((64, 1024), 0))
    chosen_z = onehot((cell & 127) == iota((128, 1024), 0))
    mask = nt(chosen_xy, chosen_z).astype(BF)
    for k in range(4):
        m4[k * 64:(k + 1) * 64, :] = mask
    gmat[...] = onehot((iota((128, 128), 0) >> 3) == (iota((128, 128), 1) & 15))
    rmat[...] = onehot(iota((32, 256), 0) == (iota((32, 256), 1) >> 3))

    @pl.loop(0, 8)
    def _(k):
        rows = pl.ds(pl.multiple_of(k * 128, 128), 128)
        pbuf[rows, :] = onehot((cell >> 3) == iota((128, 1024), 0) + k * 128)

    for k in range(GROUPS):
        cin[k].wait()

        @pl.loop(k * BATCH, (k + 1) * BATCH)
        def _(q):
            rows = pl.ds(pl.multiple_of(q * 256, 256), 256)
            t = mm(v0[rows, :] * m4[...], gmat[...])
            same = (iota((256, 128), 0) & 7) == (iota((256, 128), 1) >> 4)
            t = jnp.where(same, t, 0.0).astype(BF)
            cbuf[pl.ds(pl.multiple_of(q * 32, 32), 32), :] = mm(rmat[...], t)

    for x in range(8):
        c2[:, x * 128:(x + 1) * 128] = cbuf[pl.ds(x, 128, stride=8), :].astype(BF)
    for h in range(2):
        tr[r, h] = mm(c2[...], pbuf[:, h * 512:(h + 1) * 512]).astype(BF)

    pl.semaphore_wait(barrier, peers)

    to_right = [rcopy(tr.at[r, h], tr.at[r, h], ts_s.at[0, h], ts_r.at[0, h], {"row": right}) for h in range(2)]
    to_left = [rcopy(tr.at[r, h], tr.at[r, h], ts_s.at[1, h], ts_r.at[1, h], {"row": left}) for h in range(2)]
    from_left = [rcopy(tr.at[left, h], tr.at[left, h], ts_s.at[0, h], ts_r.at[0, h], {"row": right}) for h in range(2)]
    from_right = [rcopy(tr.at[right, h], tr.at[right, h], ts_s.at[1, h], ts_r.at[1, h], {"row": left}) for h in range(2)]
    relay_right = rcopy(tr.at[left, 0], tr.at[left, 0], ts_s.at[2, 0], ts_r.at[2, 0], {"row": right})
    relay_left = rcopy(tr.at[right, 1], tr.at[right, 1], ts_s.at[2, 1], ts_r.at[2, 1], {"row": left})
    from_far = [
        rcopy(tr.at[far, 0], tr.at[far, 0], ts_s.at[2, 0], ts_r.at[2, 0], {"row": right}),
        rcopy(tr.at[far, 1], tr.at[far, 1], ts_s.at[2, 1], ts_r.at[2, 1], {"row": left}),
    ]
    to_right[0].start()
    to_left[1].start()
    to_right[1].start()
    to_left[0].start()

    p, q = iota((128, 256), 0), iota((128, 256), 1)
    d, o = p >> 5, p & 7
    qx, qy = (q >> 3) & 7, q & 7
    hit = jnp.where(
        d < 2,
        jnp.where(qx == d * 7, jnp.where(qy == o, 1.0, 0.0), 0.0),
        jnp.where(qy == (d - 2) * 7, jnp.where(qx == o, 1.0, 0.0), 0.0),
    )
    ebd[...] = jnp.where(((p >> 3) & 3) == (q >> 6), hit, 0.0).astype(BF)
    p, q = iota((256, 128), 0), iota((256, 128), 1)
    d, o = q >> 5, q & 7
    px, py = (p >> 3) & 7, p & 7
    hit = jnp.where(
        d < 2,
        jnp.where(px == d * 7, jnp.where(py == o, 1.0, 0.0), 0.0),
        jnp.where(py == (d - 2) * 7, jnp.where(px == o, 1.0, 0.0), 0.0),
    )
    hbd[...] = jnp.where(((q >> 3) & 3) == (p >> 6), hit, 0.0).astype(BF)
    p, q = iota((256, 256), 0), iota((256, 256), 1)
    dx = jnp.abs(((p >> 3) & 7) - ((q >> 3) & 7))
    dy = jnp.abs((p & 7) - (q & 7))
    abd[...] = jnp.where((p >> 6) == (q >> 6), jnp.where(dx + dy == 1, 1.0, 0.0), 0.0).astype(BF)
    smat[...] = onehot(jnp.abs(iota((128, 128), 0) - iota((128, 128), 1)) == 1)
    wz[...] = onehot(iota((16, 128), 1) == jnp.where(iota((16, 128), 0) < 2, iota((16, 128), 0) * 127, -1))

    w = OMEGA / (6.0 + coef_ref[...])
    for k in range(4):
        w4[k * 64:(k + 1) * 64, :] = w

    row8 = iota((8, 128), 0) & 3
    cells = jnp.zeros((8, 128), I32)
    weight = jnp.zeros((8, 128), F32)
    number = iota((64, 128), 0) * 128 + iota((64, 128), 1)
    for k in range(4):
        fc = fcell_ref[k]
        wk = jnp.sum(jnp.where(number == fc, w, 0.0), axis=(0, 1), keepdims=True)
        cells = jnp.where(row8 == k, fc, cells)
        weight = jnp.where(row8 == k, wk, weight)
    cinfo[...] = cells.astype(F32)
    for d in range(6):
        @pl.when(exists[d])
        def _(d=d):
            rcopy(cinfo, cnb.at[d ^ 1], i_s.at[d], i_r.at[d ^ 1], nbid[d]).start()

    for d in range(6):
        @pl.when(jnp.logical_not(exists[d]))
        def _(d=d):
            cnb[d] = jnp.zeros((8, 128), F32)
            gnb[d] = jnp.zeros((8, 128), F32)
            for s in range(3):
                if d < 4:
                    @pl.loop(0, 8)
                    def _(k, s=s):
                        hb[s, d, pl.ds(pl.multiple_of(k * 128, 128), 128), :] = jnp.zeros((128, 128), BF)
                else:
                    zh[s, d - 4] = jnp.zeros((NB, 256), F32)

    def halo(s, d, k):
        if d < 4:
            rows = pl.ds(pl.multiple_of(k * 256, 256), 256)
            src, dst = fs.at[s, d, rows], hb.at[s, d ^ 1, rows]
        else:
            rows = pl.ds(pl.multiple_of(k * 8, 8), 8)
            src, dst = zs.at[s, d - 4, rows], zh.at[s, (d ^ 1) - 4, rows]
        return rcopy(src, dst, hs_s.at[s, d, k], hs_r.at[s, d ^ 1, k], nbid[d])

    def send_halos(s, k):
        for d in (2, 3, 0, 1, 4, 5):
            @pl.when(exists[d])
            def _(d=d):
                halo(s, d, k).start()

    def wait_halos(s, k):
        for d in range(6):
            @pl.when(exists[d])
            def _(d=d):
                if d < 4:
                    rows = pl.ds(pl.multiple_of(k * 256, 256), 256)
                    dst = hb.at[s, d, rows]
                else:
                    rows = pl.ds(pl.multiple_of(k * 8, 8), 8)
                    dst = zh.at[s, d - 4, rows]
                rcopy(dst, dst, hs_s.at[s, d, k], hs_r.at[s, d, k], nbid[d]).wait_recv()

    def faces(s, q, v):
        f = mm(ebd[...], v).astype(BF)
        rows = pl.ds(pl.multiple_of(q * 32, 32), 32)
        for d in range(4):
            fs[s, d, rows, :] = f[d * 32:(d + 1) * 32, :]
        zf = nt(wz[...], v)
        for d in range(2):
            zs[s, d, pl.ds(q, 1), :] = zf[d:d + 1, :]

    def sweep(s, q, vin, extra_rows, extra_cols):
        rows = pl.ds(pl.multiple_of(q * 256, 256), 256)
        hrows = pl.ds(pl.multiple_of(q * 32, 32), 32)
        v = vin[rows, :]
        around = jnp.concatenate([hb[s, d, hrows, :] for d in range(4)], axis=0)
        rid = iota((16, 256), 0)
        zz = jnp.where(rid == 0, zh[s, 0, pl.ds(q, 1), :], jnp.where(rid == 1, zh[s, 1, pl.ds(q, 1), :], 0.0))
        lhs, rhs = zz.astype(BF), wz[...]
        if extra_rows is not None:
            lhs = jnp.concatenate([lhs, extra_rows], axis=0)
            rhs = jnp.concatenate([rhs, extra_cols], axis=0)
        acc = mm(abd[...], v) + mm(hbd[...], around) + mm(v, smat[...]) + tn(lhs, rhs)
        return 0.2 * v.astype(F32) + w4[...] * (ld[rows, :].astype(F32) + acc)

    def spread(q, values, places):
        pick = onehot(iota((128, 256), 0) == 4 * q + (iota((128, 256), 1) >> 6))
        return (mm(values, pick) * places).astype(BF)

    def sweep1(k):
        wait_halos(0, k)

        @pl.loop(k * BATCH, (k + 1) * BATCH)
        def _(q):
            new = sweep(0, q, v0, None, None).astype(BF)
            v1[pl.ds(pl.multiple_of(q * 256, 256), 256), :] = new
            faces(1, q, new)
        send_halos(1, k)

    for k in range(GROUPS):
        @pl.loop(k * BATCH, (k + 1) * BATCH)
        def _(q):
            faces(0, q, v0[pl.ds(pl.multiple_of(q * 256, 256), 256), :])
        send_halos(0, k)
        if k == 1:
            from_left[0].wait_recv()
            relay_right.start()
            from_right[1].wait_recv()
            relay_left.start()

    for k in range(GROUPS):
        cld[k].wait()

    def product(o):
        csb[o].wait()
        src = (r + o) % 4
        return nt(sb[o, :, 0:512], tr[src, 0]) + nt(sb[o, :, 512:1024], tr[src, 1])

    part[...] = product(0)
    from_left[1].wait_recv()
    part[...] += product(3)
    from_right[0].wait_recv()
    part[...] += product(1)
    sweep1(0)
    from_far[0].wait_recv()
    from_far[1].wait_recv()
    total = (part[...] + product(2)).reshape(32, 8, 128)
    low, high = total[:, 0:4, :], total[:, 4:8, :]
    first = b == 0
    cown[...] = jnp.where(first, low, high)
    csend[...] = jnp.where(first, high, low)
    core = rcopy(csend, crecv, c_s, c_r, {"gz": g + 1 - 2 * b})
    core.start()
    sweep1(1)
    core.wait_recv()
    qbuf[...] = cown[...] + crecv[...]
    yrecv[y] = qbuf[pl.ds(y * 8, 8)]
    ycopies = []
    for o in range(1, 4):
        peer = (y + o) % 4
        cp = rcopy(qbuf.at[pl.ds(peer * 8, 8)], yrecv.at[y], y_s.at[o - 1], y_r.at[o - 1], {"col": peer * 4 + zl})
        cp.start()
        ycopies.append(cp)
    sweep1(2)
    for o in range(1, 4):
        peer = (y + 4 - o) % 4
        rcopy(yrecv.at[peer], yrecv.at[peer], y_s.at[o - 1], y_r.at[o - 1], {"col": peer * 4 + zl}).wait_recv()
    zsend[...] = (yrecv[0] + yrecv[1]) + (yrecv[2] + yrecv[3])
    zrecv[jz] = zsend[jz]
    zcopies = []
    for o in range(1, 8):
        peer = (jz + o) % 8
        cp = rcopy(zsend.at[peer], zrecv.at[jz], z_s.at[o - 1], z_r.at[o - 1], zdev(o))
        cp.start()
        zcopies.append(cp)
    sweep1(3)

    for d in range(6):
        @pl.when(exists[d])
        def _(d=d):
            rcopy(cnb.at[d], cnb.at[d], i_s.at[d], i_r.at[d], nbid[d]).wait_recv()
    mine = iota((8, 128), 0) < 4
    lane = iota((8, 256), 1) & 63
    for k in range(7):
        if k == 0:
            tx, ty, tz = cells >> 10, (cells >> 7) & 7, cells & 127
        else:
            ox, oy, oz = OFFS[k - 1]
            other = cnb[k - 1].astype(I32)
            at = jnp.where(mine, cells, other)
            tx = (at >> 10) + jnp.where(mine, ox, 7 * ox)
            ty = ((at >> 7) & 7) + jnp.where(mine, oy, 7 * oy)
            tz = (at & 127) + jnp.where(mine, oz, 127 * oz)
        txy = jnp.where((tx >= 0) & (tx < 8) & (ty >= 0) & (ty < 8), tx * 8 + ty, -1)
        tz = jnp.where((tz >= 0) & (tz < 128), tz, -1)
        spots = jnp.where(jnp.concatenate([txy, txy], axis=1) == lane, 1.0, 0.0)
        cols = jnp.where(tz == iota((8, 128), 1), 1.0, 0.0)
        for part_ in range(2):
            lmask[part_ * 56 + k * 8:part_ * 56 + k * 8 + 8, :] = spots
            zmask[part_ * 56 + k * 8:part_ * 56 + k * 8 + 8, :] = cols

    for o in range(1, 8):
        peer = (jz + 8 - o) % 8
        rcopy(zrecv.at[peer], zrecv.at[peer], z_s.at[o - 1], z_r.at[o - 1], zdev(8 - o)).wait_recv()
    own = zrecv[0]
    for j in range(1, 8):
        own = own + zrecv[j]
    fbuf[...] = own
    own8 = jnp.concatenate([own, own], axis=0)
    gvals = weight * own8
    gbuf[...] = gvals
    for d in range(6):
        @pl.when(exists[d])
        def _(d=d):
            rcopy(gbuf, gnb.at[d ^ 1], g_s.at[d], g_r.at[d ^ 1], nbid[d]).start()
    fall[g] = own
    fcopies = []
    for o in range(1, 4):
        cp = rcopy(fbuf, fall.at[g], f_s.at[o - 1], f_r.at[o - 1], {"gz": (g + o) % 4})
        cp.start()
        fcopies.append(cp)

    for d in range(6):
        @pl.when(exists[d])
        def _(d=d):
            rcopy(gnb.at[d], gnb.at[d], g_s.at[d], g_r.at[d], nbid[d]).wait_recv()

    def split(values):
        hi = values.astype(BF).astype(F32)
        return hi, values - hi

    centre = jnp.where(mine, own8, 0.0)
    pieces = [1.2 * centre] + [jnp.where(mine, gvals, gnb[d]) for d in range(6)]
    for k in range(7):
        hi, lo = split(pieces[k])
        val[k * 8:k * 8 + 8, :] = hi
        val[56 + k * 8:56 + k * 8 + 8, :] = lo
    hi, lo = split(centre)
    val3[0:8, :] = hi
    val3[8:16, :] = lo

    @pl.loop(0, GROUPS)
    def _(k):
        wait_halos(1, k)

        @pl.loop(k * BATCH, (k + 1) * BATCH)
        def _(q):
            rows = spread(q, val[...].astype(BF), lmask[...])
            new = sweep(1, q, v1, rows, zmask[...].astype(BF)).astype(BF)
            v2[pl.ds(pl.multiple_of(q * 256, 256), 256), :] = new
            faces(2, q, new)
        send_halos(2, k)

    def put(k):
        rows = pl.ds(pl.multiple_of(k * 2048, 2048), 2048)
        return pltpu.make_async_copy(v3.at[rows], out_hbm.at[rows], outsem.at[k])

    @pl.loop(0, GROUPS)
    def _(k):
        wait_halos(2, k)

        @pl.loop(k * BATCH, (k + 1) * BATCH)
        def _(q):
            places = jnp.concatenate([lmask[0:8, :], lmask[0:8, :]], axis=0)
            cols = jnp.concatenate([zmask[0:8, :], zmask[0:8, :]], axis=0).astype(BF)
            rows = spread(q, val3[...].astype(BF), places)
            new = sweep(2, q, v2, rows, cols).astype(BF)
            v3[pl.ds(pl.multiple_of(q * 256, 256), 256), :] = new
        put(k).start()

    for o in range(1, 4):
        peer = (g + 4 - o) % 4
        rcopy(fall.at[peer], fall.at[peer], f_s.at[o - 1], f_r.at[o - 1], {"gz": peer}).wait_recv()
    sel = jnp.where(iota((32, 128), 1) == g * 32 + iota((32, 128), 0), 1.0, 0.0)
    rows16 = jnp.concatenate([fall[0], fall[1], fall[2], fall[3]], axis=0)
    flux_ref[...] = nt(sel, rows16, precision=lax.Precision.HIGHEST)

    for cp in to_right + to_left + [relay_right, relay_left, core] + ycopies + zcopies + fcopies:
        cp.wait_send()
    for d in range(6):
        @pl.when(exists[d])
        def _(d=d):
            rcopy(cinfo, cnb.at[d ^ 1], i_s.at[d], i_r.at[d ^ 1], nbid[d]).wait_send()
            rcopy(gbuf, gnb.at[d ^ 1], g_s.at[d], g_r.at[d ^ 1], nbid[d]).wait_send()
            for s in range(3):
                @pl.loop(0, GROUPS)
                def _(k):
                    halo(s, d, k).wait_send()
    for k in range(GROUPS):
        put(k).wait()


def per_device(volume_field, volume_load, coefficient, surface_block, trace_cell, flux_cell):
    side_count, first_span, second_span, third_span = volume_field.shape
    rows = side_count * first_span * second_span
    vm = pltpu.VMEM
    dma = pltpu.SemaphoreType.DMA
    scratch = [
        vm((rows, 128), BF), vm((rows, 128), BF), vm((rows, 128), BF), vm((rows, 128), BF), vm((rows, 128), BF),
        vm((4, 256, 1024), BF), vm((4, 2, 128, 512), BF), vm((256, 128), F32),
        vm((3, 4, 1024, 128), BF), vm((3, 4, 1024, 128), BF), vm((3, 2, NB, 256), F32), vm((3, 2, NB, 256), F32),
        vm((256, 256), BF), vm((256, 128), BF), vm((128, 256), BF), vm((128, 128), BF), vm((128, 128), BF),
        vm((32, 256), BF), vm((16, 128), BF), vm((256, 128), BF), vm((1024, 128), F32), vm((128, 1024), BF),
        vm((1024, 1024), BF),
        vm((256, 128), F32), vm((32, 4, 128), F32), vm((32, 4, 128), F32), vm((32, 4, 128), F32),
        vm((32, 4, 128), F32), vm((4, 8, 4, 128), F32), vm((8, 4, 128), F32), vm((8, 4, 128), F32),
        vm((4, 128), F32), vm((4, 4, 128), F32),
        vm((8, 128), F32), vm((6, 8, 128), F32), vm((8, 128), F32), vm((6, 8, 128), F32),
        vm((112, 256), F32), vm((112, 128), F32), vm((112, 128), F32), vm((16, 128), F32),
        dma((2, GROUPS)), dma((4,)), dma((GROUPS,)), dma((3, 6, GROUPS)), dma((3, 6, GROUPS)),
        dma((3, 2)), dma((3, 2)), dma, dma, dma((3,)), dma((3,)), dma((7,)), dma((7,)),
        dma((3,)), dma((3,)), dma((6,)), dma((6,)), dma((6,)), dma((6,)),
    ]
    anywhere = pl.BlockSpec(memory_space=pl.ANY)
    local = pl.BlockSpec(memory_space=pltpu.VMEM)
    new_field, surface_flux = pl.pallas_call(
        kernel,
        out_shape=(jax.ShapeDtypeStruct((rows, 128), BF), jax.ShapeDtypeStruct((32, 16), F32)),
        in_specs=[anywhere, anywhere, local, anywhere, local, pl.BlockSpec(memory_space=pltpu.SMEM)],
        out_specs=(anywhere, local),
        scratch_shapes=scratch,
        compiler_params=pltpu.CompilerParams(
            collective_id=0, has_side_effects=True, vmem_limit_bytes=60 * 1024 * 1024
        ),
    )(
        volume_field.reshape(rows, 128),
        volume_load.reshape(rows, 128),
        coefficient.reshape(64, 128),
        surface_block,
        trace_cell.reshape(1, 1024),
        flux_cell.reshape(4),
    )
    return new_field.reshape(volume_field.shape), surface_flux


def solution(mesh):
    in_specs = (
        P(None, "row", "col", "gz"),
        P(None, "row", "col", "gz"),
        P("row", "col", "gz"),
        P("row", "col"),
        P("row", "col", "gz", None),
        P("row", "col", "gz", None),
    )
    out_specs = (P(None, "row", "col", "gz"), P("gz", ("row", "col")))
    return jax.shard_map(
        per_device, mesh=mesh, in_specs=in_specs, out_specs=out_specs, check_vma=False
    )
```

time: 317 us -> 86.9 us (0.27)
  the two profiles are of different devices: /device:TPU:11 before, /device:TPU:1 now
where the time goes in v1:
time: 86.9 us; the launch traced here: 86.6 us
  Pallas kernels  81.5 us (94%)
  local copies, waits for them, and re-layouts  4.47 us (5%)
    pallas_call x1, Pallas kernels, per_device(): pl.pallas_call(kernel, out_shape=(jax.ShapeDtypeStruct((rows, 128), BF),...  81.5 us
    unnamed x2, local copies, waits for them, and re-layouts  4.47 us

profile of v1, /device:TPU:1, one launch (start us, length us, event | category | flops | bytes accessed | tf_op | source)
XLA Modules:
  0.0 86.6 jit_solution(11471771291477189101)
XLA Ops:
  0.6 81.5 %shard_map.77 = (bf16[8192,128]{1,0:T(8,128)(2,1)}, f32[32,16]{1,0:T(8,128)}) custom-call(bf16[8192,128]{1,0:T(8,128)(2,1)} %bitcast.7, bf16[8192,128]{1,0:T(8,128)(2,1)} %bitcast.8, f32[64,128]{1,0:T(8,128)} %bitcast.9, bf16[256,16384]{1,0:T(8,128)(2,1)} %sb_hbm.1, s32[1,1024]{1,0:T(1,128)} %bitcast.10, s32[4]{0:T(128)} %bitcast.11), custom_call_target="tpu_custom_call" | custom-call | tf_op jit(solution)/shard_map/pallas_call | solution.py:473
  82.2 1.4 %copy.8 = f32[32,16]{0,1:T(8,128)} copy(f32[32,16]{1,0:T(8,128)} %get-tuple-element.7) | data formatting | bytes 4096
  83.6 3.1 %copy.10 = bf16[128,8,8,128]{3,2,1,0:T(8,128)(2,1)} copy(bf16[128,8,8,128]{3,2,1,0:T(8,128)(2,1)} %bitcast.6) | data formatting | bytes 4194304

commit v2 on v1

--- a/solution.py
+++ b/solution.py
@@ -13,8 +13,9 @@
 I32 = jnp.int32
 OMEGA = 0.8
 GROUPS = 4
-BATCH = 8
-NB = GROUPS * BATCH
+UNITS = 4
+STEP = 2
+NB = GROUPS * UNITS * 2
 OFFS = ((-1, 0, 0), (1, 0, 0), (0, -1, 0), (0, 1, 0), (0, 0, -1), (0, 0, 1))
 
 
@@ -42,9 +43,9 @@
     field_hbm, load_hbm, coef_ref, sb_hbm, tcell_ref, fcell_ref,
     out_hbm, flux_ref,
     v0, ld, v1, v2, v3, sb, tr, w4, hb, fs, zh, zs,
-    abd, hbd, ebd, smat, gmat, rmat, wz, m4, cbuf, c2, pbuf,
+    ah, emat, ss, gg, rmat, wz, uu, m4, ymask, cbuf, c2, pbuf,
     part, cown, csend, crecv, qbuf, yrecv, zsend, zrecv, fbuf, fall,
-    gbuf, gnb, cinfo, cnb, lmask, zmask, val, val3,
+    gbuf, gnb, cinfo, cnb, lmask, zcols, zcols3, val, val3,
     insem, sbsem, outsem, hs_s, hs_r, ts_s, ts_r, c_s, c_r, y_s, y_r, z_s, z_r,
     f_s, f_r, g_s, g_r, i_s, i_r,
 ):
@@ -112,7 +113,9 @@
     mask = nt(chosen_xy, chosen_z).astype(BF)
     for k in range(4):
         m4[k * 64:(k + 1) * 64, :] = mask
-    gmat[...] = onehot((iota((128, 128), 0) >> 3) == (iota((128, 128), 1) & 15))
+    p, q = iota((256, 256), 0), iota((256, 256), 1)
+    gg[...] = jnp.where((p >> 7) == (q >> 7), jnp.where(((p & 127) >> 3) == (q & 15), 1.0, 0.0), 0.0).astype(BF)
+    ymask[...] = onehot((p & 7) == ((q & 127) >> 4))
     rmat[...] = onehot(iota((32, 256), 0) == (iota((32, 256), 1) >> 3))
 
     @pl.loop(0, 8)
@@ -123,13 +126,16 @@
     for k in range(GROUPS):
         cin[k].wait()
 
-        @pl.loop(k * BATCH, (k + 1) * BATCH)
-        def _(q):
-            rows = pl.ds(pl.multiple_of(q * 256, 256), 256)
-            t = mm(v0[rows, :] * m4[...], gmat[...])
-            same = (iota((256, 128), 0) & 7) == (iota((256, 128), 1) >> 4)
-            t = jnp.where(same, t, 0.0).astype(BF)
-            cbuf[pl.ds(pl.multiple_of(q * 32, 32), 32), :] = mm(rmat[...], t)
+        @pl.loop(k * UNITS // STEP, (k + 1) * UNITS // STEP)
+        def _(i):
+            for j in range(STEP):
+                u = i * STEP + j
+                a = v0[pl.ds(pl.multiple_of(u * 512, 512), 256), :] * m4[...]
+                bb = v0[pl.ds(pl.multiple_of(u * 512 + 256, 256), 256), :] * m4[...]
+                t = mm(jnp.concatenate([a, bb], axis=1), gg[...]).astype(BF) * ymask[...]
+                t = mm(rmat[...], t)
+                cbuf[pl.ds(pl.multiple_of(u * 64, 64), 32), :] = t[:, :128]
+                cbuf[pl.ds(pl.multiple_of(u * 64 + 32, 32), 32), :] = t[:, 128:]
 
     for x in range(8):
         c2[:, x * 128:(x + 1) * 128] = cbuf[pl.ds(x, 128, stride=8), :].astype(BF)
@@ -153,33 +159,36 @@
     to_right[1].start()
     to_left[0].start()
 
-    p, q = iota((128, 256), 0), iota((128, 256), 1)
-    d, o = p >> 5, p & 7
+    p, q = iota((64, 128), 0), iota((64, 128), 1)
+    d, o = p >> 4, p & 7
     qx, qy = (q >> 3) & 7, q & 7
     hit = jnp.where(
         d < 2,
         jnp.where(qx == d * 7, jnp.where(qy == o, 1.0, 0.0), 0.0),
         jnp.where(qy == (d - 2) * 7, jnp.where(qx == o, 1.0, 0.0), 0.0),
     )
-    ebd[...] = jnp.where(((p >> 3) & 3) == (q >> 6), hit, 0.0).astype(BF)
-    p, q = iota((256, 128), 0), iota((256, 128), 1)
-    d, o = q >> 5, q & 7
+    emat[...] = jnp.where(((p >> 3) & 1) == (q >> 6), hit, 0.0).astype(BF)
+    p, q = iota((128, 256), 0), iota((128, 256), 1)
     px, py = (p >> 3) & 7, p & 7
+    dx = jnp.abs(px - ((q >> 3) & 7))
+    dy = jnp.abs(py - (q & 7))
+    inside = jnp.where((p >> 6) == ((q >> 6) & 1), jnp.where(dx + dy == 1, 1.0, 0.0), 0.0)
+    d, o = (q >> 4) & 7, q & 7
     hit = jnp.where(
         d < 2,
         jnp.where(px == d * 7, jnp.where(py == o, 1.0, 0.0), 0.0),
         jnp.where(py == (d - 2) * 7, jnp.where(px == o, 1.0, 0.0), 0.0),
     )
-    hbd[...] = jnp.where(((q >> 3) & 3) == (p >> 6), hit, 0.0).astype(BF)
+    hit = jnp.where(((q >> 3) & 1) == (p >> 6), hit, 0.0)
+    ah[...] = jnp.where(q < 128, inside, hit)[:, :192].astype(BF)
     p, q = iota((256, 256), 0), iota((256, 256), 1)
-    dx = jnp.abs(((p >> 3) & 7) - ((q >> 3) & 7))
-    dy = jnp.abs((p & 7) - (q & 7))
-    abd[...] = jnp.where((p >> 6) == (q >> 6), jnp.where(dx + dy == 1, 1.0, 0.0), 0.0).astype(BF)
-    smat[...] = onehot(jnp.abs(iota((128, 128), 0) - iota((128, 128), 1)) == 1)
+    ss[...] = jnp.where((p >> 7) == (q >> 7), jnp.where(jnp.abs(p - q) == 1, 1.0, 0.0), 0.0).astype(BF)
+    p, q = iota((16, 256), 0), iota((16, 256), 1)
+    uu[...] = jnp.where(p < 4, jnp.where(q == (p >> 1) * 128 + (p & 1) * 127, 1.0, 0.0), 0.0).astype(BF)
     wz[...] = onehot(iota((16, 128), 1) == jnp.where(iota((16, 128), 0) < 2, iota((16, 128), 0) * 127, -1))
 
     w = OMEGA / (6.0 + coef_ref[...])
-    for k in range(4):
+    for k in range(2):
         w4[k * 64:(k + 1) * 64, :] = w
 
     row8 = iota((8, 128), 0) & 3
@@ -237,47 +246,69 @@
                     dst = zh.at[s, d - 4, rows]
                 rcopy(dst, dst, hs_s.at[s, d, k], hs_r.at[s, d, k], nbid[d]).wait_recv()
 
-    def faces(s, q, v):
-        f = mm(ebd[...], v).astype(BF)
-        rows = pl.ds(pl.multiple_of(q * 32, 32), 32)
-        for d in range(4):
-            fs[s, d, rows, :] = f[d * 32:(d + 1) * 32, :]
-        zf = nt(wz[...], v)
-        for d in range(2):
-            zs[s, d, pl.ds(q, 1), :] = zf[d:d + 1, :]
-
-    def sweep(s, q, vin, extra_rows, extra_cols):
-        rows = pl.ds(pl.multiple_of(q * 256, 256), 256)
-        hrows = pl.ds(pl.multiple_of(q * 32, 32), 32)
-        v = vin[rows, :]
-        around = jnp.concatenate([hb[s, d, hrows, :] for d in range(4)], axis=0)
+    def faces(s, u, pairs):
+        for i, pair in enumerate(pairs):
+            f = mm(emat[...], pair).astype(BF)
+            for j in range(2):
+                rows = pl.ds(pl.multiple_of(u * 64 + i * 32 + j * 16, 16), 16)
+                for d in range(4):
+                    fs[s, d, rows, :] = f[d * 16:(d + 1) * 16, j * 128:(j + 1) * 128]
+            v = jnp.concatenate([pair[:, :128], pair[:, 128:]], axis=0)
+            zf = nt(wz[...], v)
+            for d in range(2):
+                zs[s, d, pl.ds(2 * u + i, 1), :] = zf[d:d + 1, :]
+
+    def sweep(s, u, vin, vout, more_rows, cols):
+        v = [vin[pl.ds(pl.multiple_of(u * 512 + i * 128, 128), 128), :] for i in range(4)]
         rid = iota((16, 256), 0)
-        zz = jnp.where(rid == 0, zh[s, 0, pl.ds(q, 1), :], jnp.where(rid == 1, zh[s, 1, pl.ds(q, 1), :], 0.0))
-        lhs, rhs = zz.astype(BF), wz[...]
-        if extra_rows is not None:
-            lhs = jnp.concatenate([lhs, extra_rows], axis=0)
-            rhs = jnp.concatenate([rhs, extra_cols], axis=0)
-        acc = mm(abd[...], v) + mm(hbd[...], around) + mm(v, smat[...]) + tn(lhs, rhs)
-        return 0.2 * v.astype(F32) + w4[...] * (ld[rows, :].astype(F32) + acc)
-
-    def spread(q, values, places):
-        pick = onehot(iota((128, 256), 0) == 4 * q + (iota((128, 256), 1) >> 6))
-        return (mm(values, pick) * places).astype(BF)
+        ends = jnp.zeros((16, 256), F32)
+        for i in range(2):
+            for d in range(2):
+                ends = jnp.where(rid == 2 * i + d, zh[s, d, pl.ds(2 * u + i, 1), :], ends)
+        lhs = jnp.concatenate([ends] + more_rows, axis=0).astype(BF)
+        t = tn(lhs, cols)
+        wide = jnp.concatenate([jnp.concatenate(v[:2], axis=0), jnp.concatenate(v[2:], axis=0)], axis=1)
+        z = mm(wide, ss[...]) + t
+        pairs = []
+        for i in range(2):
+            sides = []
+            for j in range(2):
+                rows = pl.ds(pl.multiple_of(u * 64 + i * 32 + j * 16, 16), 16)
+                sides.append(jnp.concatenate([v[2 * i + j]] + [hb[s, d, rows, :] for d in range(4)], axis=0))
+            xy = mm(ah[...], jnp.concatenate(sides, axis=1))
+            new = []
+            for j in range(2):
+                rows = pl.ds(pl.multiple_of(u * 512 + (2 * i + j) * 128, 128), 128)
+                acc = xy[:, j * 128:(j + 1) * 128] + z[j * 128:(j + 1) * 128, i * 128:(i + 1) * 128]
+                acc = acc + ld[rows, :].astype(F32)
+                n = (0.2 * v[2 * i + j].astype(F32) + w4[...] * acc).astype(BF)
+                vout[rows, :] = n
+                new.append(n)
+            pairs.append(jnp.concatenate(new, axis=1))
+        return pairs
+
+    def spread(u, values, places):
+        pick = onehot(iota((128, 512), 0) == 8 * u + (iota((128, 512), 1) >> 6))
+        m = mm(values, pick)
+        return [m[:, :256] * places, m[:, 256:] * places]
 
     def sweep1(k):
         wait_halos(0, k)
 
-        @pl.loop(k * BATCH, (k + 1) * BATCH)
-        def _(q):
-            new = sweep(0, q, v0, None, None).astype(BF)
-            v1[pl.ds(pl.multiple_of(q * 256, 256), 256), :] = new
-            faces(1, q, new)
+        @pl.loop(k * UNITS // STEP, (k + 1) * UNITS // STEP)
+        def _(i):
+            for j in range(STEP):
+                u = i * STEP + j
+                faces(1, u, sweep(0, u, v0, v1, [], uu[...]))
         send_halos(1, k)
 
     for k in range(GROUPS):
-        @pl.loop(k * BATCH, (k + 1) * BATCH)
-        def _(q):
-            faces(0, q, v0[pl.ds(pl.multiple_of(q * 256, 256), 256), :])
+        @pl.loop(k * UNITS // STEP, (k + 1) * UNITS // STEP)
+        def _(i):
+            for j in range(STEP):
+                u = i * STEP + j
+                v = [v0[pl.ds(pl.multiple_of(u * 512 + n * 128, 128), 128), :] for n in range(4)]
+                faces(0, u, [jnp.concatenate(v[:2], axis=1), jnp.concatenate(v[2:], axis=1)])
         send_halos(0, k)
         if k == 1:
             from_left[0].wait_recv()
@@ -352,9 +383,18 @@
         tz = jnp.where((tz >= 0) & (tz < 128), tz, -1)
         spots = jnp.where(jnp.concatenate([txy, txy], axis=1) == lane, 1.0, 0.0)
         cols = jnp.where(tz == iota((8, 128), 1), 1.0, 0.0)
-        for part_ in range(2):
-            lmask[part_ * 56 + k * 8:part_ * 56 + k * 8 + 8, :] = spots
-            zmask[part_ * 56 + k * 8:part_ * 56 + k * 8 + 8, :] = cols
+        lmask[k * 8:k * 8 + 8, :] = spots
+        zcols[16 + k * 8:24 + k * 8, 0:128] = cols
+        zcols[16 + k * 8:24 + k * 8, 128:256] = jnp.zeros((8, 128), F32)
+        zcols[72 + k * 8:80 + k * 8, 0:128] = jnp.zeros((8, 128), F32)
+        zcols[72 + k * 8:80 + k * 8, 128:256] = cols
+        if k == 0:
+            zcols3[16:24, 0:128] = cols
+            zcols3[16:24, 128:256] = jnp.zeros((8, 128), F32)
+            zcols3[24:32, 0:128] = jnp.zeros((8, 128), F32)
+            zcols3[24:32, 128:256] = cols
+    zcols[0:16, :] = uu[...].astype(F32)
+    zcols3[0:16, :] = uu[...].astype(F32)
 
     for o in range(1, 8):
         peer = (jz + 8 - o) % 8
@@ -386,26 +426,23 @@
         hi = values.astype(BF).astype(F32)
         return hi, values - hi
 
-    centre = jnp.where(mine, own8, 0.0)
-    pieces = [1.2 * centre] + [jnp.where(mine, gvals, gnb[d]) for d in range(6)]
-    for k in range(7):
-        hi, lo = split(pieces[k])
-        val[k * 8:k * 8 + 8, :] = hi
-        val[56 + k * 8:56 + k * 8 + 8, :] = lo
-    hi, lo = split(centre)
-    val3[0:8, :] = hi
-    val3[8:16, :] = lo
+    hi, lo = split(1.2 * own8)
+    val[0:8, :] = jnp.where(mine, hi, lo)
+    for d in range(6):
+        val[8 + d * 8:16 + d * 8, :] = jnp.where(mine, gvals, gnb[d])
+    hi, lo = split(own8)
+    val3[...] = jnp.where(mine, hi, lo)
 
     @pl.loop(0, GROUPS)
     def _(k):
         wait_halos(1, k)
 
-        @pl.loop(k * BATCH, (k + 1) * BATCH)
-        def _(q):
-            rows = spread(q, val[...].astype(BF), lmask[...])
-            new = sweep(1, q, v1, rows, zmask[...].astype(BF)).astype(BF)
-            v2[pl.ds(pl.multiple_of(q * 256, 256), 256), :] = new
-            faces(2, q, new)
+        @pl.loop(k * UNITS // STEP, (k + 1) * UNITS // STEP)
+        def _(i):
+            for j in range(STEP):
+                u = i * STEP + j
+                rows = spread(u, val[...].astype(BF), lmask[...])
+                faces(2, u, sweep(1, u, v1, v2, rows, zcols[...].astype(BF)))
         send_halos(2, k)
 
     def put(k):
@@ -416,13 +453,12 @@
     def _(k):
         wait_halos(2, k)
 
-        @pl.loop(k * BATCH, (k + 1) * BATCH)
-        def _(q):
-            places = jnp.concatenate([lmask[0:8, :], lmask[0:8, :]], axis=0)
-            cols = jnp.concatenate([zmask[0:8, :], zmask[0:8, :]], axis=0).astype(BF)
-            rows = spread(q, val3[...].astype(BF), places)
-            new = sweep(2, q, v2, rows, cols).astype(BF)
-            v3[pl.ds(pl.multiple_of(q * 256, 256), 256), :] = new
+        @pl.loop(k * UNITS // STEP, (k + 1) * UNITS // STEP)
+        def _(i):
+            for j in range(STEP):
+                u = i * STEP + j
+                rows = spread(u, val3[...].astype(BF), lmask[0:8, :])
+                sweep(2, u, v2, v3, rows, zcols3[...].astype(BF))
         put(k).start()
 
     for o in range(1, 4):
@@ -454,16 +490,17 @@
     dma = pltpu.SemaphoreType.DMA
     scratch = [
         vm((rows, 128), BF), vm((rows, 128), BF), vm((rows, 128), BF), vm((rows, 128), BF), vm((rows, 128), BF),
-        vm((4, 256, 1024), BF), vm((4, 2, 128, 512), BF), vm((256, 128), F32),
+        vm((4, 256, 1024), BF), vm((4, 2, 128, 512), BF), vm((128, 128), F32),
         vm((3, 4, 1024, 128), BF), vm((3, 4, 1024, 128), BF), vm((3, 2, NB, 256), F32), vm((3, 2, NB, 256), F32),
-        vm((256, 256), BF), vm((256, 128), BF), vm((128, 256), BF), vm((128, 128), BF), vm((128, 128), BF),
-        vm((32, 256), BF), vm((16, 128), BF), vm((256, 128), BF), vm((1024, 128), F32), vm((128, 1024), BF),
+        vm((128, 192), BF), vm((64, 128), BF), vm((256, 256), BF), vm((256, 256), BF),
+        vm((32, 256), BF), vm((16, 128), BF), vm((16, 256), BF), vm((256, 128), BF), vm((256, 256), BF),
+        vm((1024, 128), F32), vm((128, 1024), BF),
         vm((1024, 1024), BF),
         vm((256, 128), F32), vm((32, 4, 128), F32), vm((32, 4, 128), F32), vm((32, 4, 128), F32),
         vm((32, 4, 128), F32), vm((4, 8, 4, 128), F32), vm((8, 4, 128), F32), vm((8, 4, 128), F32),
         vm((4, 128), F32), vm((4, 4, 128), F32),
         vm((8, 128), F32), vm((6, 8, 128), F32), vm((8, 128), F32), vm((6, 8, 128), F32),
-        vm((112, 256), F32), vm((112, 128), F32), vm((112, 128), F32), vm((16, 128), F32),
+        vm((56, 256), F32), vm((128, 256), F32), vm((32, 256), F32), vm((56, 128), F32), vm((8, 128), F32),
         dma((2, GROUPS)), dma((4,)), dma((GROUPS,)), dma((3, 6, GROUPS)), dma((3, 6, GROUPS)),
         dma((3, 2)), dma((3, 2)), dma, dma, dma((3,)), dma((3,)), dma((7,)), dma((7,)),
         dma((3,)), dma((3,)), dma((6,)), dma((6,)), dma((6,)), dma((6,)),

time: 86.9 us -> 69.4 us (0.80)
  the two profiles are of different devices: /device:TPU:1 before, /device:TPU:24 now
where the time goes in v2:
time: 69.4 us; the launch traced here: 69.1 us
  Pallas kernels  64 us (92%)
  local copies, waits for them, and re-layouts  4.47 us (6%)
    pallas_call x1, Pallas kernels, per_device(): pl.pallas_call(kernel, out_shape=(jax.ShapeDtypeStruct((rows, 128), BF),...  64 us
    unnamed x2, local copies, waits for them, and re-layouts  4.47 us

profile of v2, /device:TPU:24, one launch (start us, length us, event | category | flops | bytes accessed | tf_op | source)
XLA Modules:
  0.0 69.1 jit_solution(8679440107782207780)
XLA Ops:
  0.6 64.0 %shard_map.77 = (bf16[8192,128]{1,0:T(8,128)(2,1)}, f32[32,16]{1,0:T(8,128)}) custom-call(bf16[8192,128]{1,0:T(8,128)(2,1)} %bitcast.7, bf16[8192,128]{1,0:T(8,128)(2,1)} %bitcast.8, f32[64,128]{1,0:T(8,128)} %bitcast.9, bf16[256,16384]{1,0:T(8,128)(2,1)} %sb_hbm.1, s32[1,1024]{1,0:T(1,128)} %bitcast.10, s32[4]{0:T(128)} %bitcast.11), custom_call_target="tpu_custom_call" | custom-call | tf_op jit(solution)/shard_map/pallas_call | solution.py:510
  64.7 1.4 %copy.8 = f32[32,16]{0,1:T(8,128)} copy(f32[32,16]{1,0:T(8,128)} %get-tuple-element.7) | data formatting | bytes 4096
  66.1 3.1 %copy.10 = bf16[128,8,8,128]{3,2,1,0:T(8,128)(2,1)} copy(bf16[128,8,8,128]{3,2,1,0:T(8,128)(2,1)} %bitcast.6) | data formatting | bytes 4194304

commit v3 on v2

--- a/solution.py
+++ b/solution.py
@@ -13,9 +13,8 @@
 I32 = jnp.int32
 OMEGA = 0.8
 GROUPS = 4
-UNITS = 4
-STEP = 2
-NB = GROUPS * UNITS * 2
+STEPS = 2
+NB = GROUPS * STEPS * 4
 OFFS = ((-1, 0, 0), (1, 0, 0), (0, -1, 0), (0, 1, 0), (0, 0, -1), (0, 0, 1))
 
 
@@ -43,10 +42,10 @@
     field_hbm, load_hbm, coef_ref, sb_hbm, tcell_ref, fcell_ref,
     out_hbm, flux_ref,
     v0, ld, v1, v2, v3, sb, tr, w4, hb, fs, zh, zs,
-    ah, emat, ss, gg, rmat, wz, uu, m4, ymask, cbuf, c2, pbuf,
+    ah, emat, ss, gg, rmat, wz, uu, m4, ymask, cbuf, c2, pbuf, xall,
     part, cown, csend, crecv, qbuf, yrecv, zsend, zrecv, fbuf, fall,
     gbuf, gnb, cinfo, cnb, lmask, zcols, zcols3, val, val3,
-    insem, sbsem, outsem, hs_s, hs_r, ts_s, ts_r, c_s, c_r, y_s, y_r, z_s, z_r,
+    insem, ldsem, sbsem, outsem, hs_s, hs_r, ts_s, ts_r, c_s, c_r, y_s, y_r, z_s, z_r,
     f_s, f_r, g_s, g_r, i_s, i_r,
 ):
     r = lax.axis_index("row")
@@ -91,21 +90,14 @@
     cin = []
     for k in range(GROUPS):
         rows = pl.ds(k * 2048, 2048)
-        cp = pltpu.make_async_copy(field_hbm.at[rows], v0.at[rows], insem.at[0, k])
+        cp = pltpu.make_async_copy(field_hbm.at[rows], v0.at[rows], insem.at[k])
         cp.start()
         cin.append(cp)
-    csb = []
     for o in range(4):
         cols = pl.multiple_of((((r + o) % 4) * 4 + g) * 1024, 1024)
-        cp = pltpu.make_async_copy(sb_hbm.at[:, pl.ds(cols, 1024)], sb.at[o], sbsem.at[o])
-        cp.start()
-        csb.append(cp)
-    cld = []
-    for k in range(GROUPS):
-        rows = pl.ds(k * 2048, 2048)
-        cp = pltpu.make_async_copy(load_hbm.at[rows], ld.at[rows], insem.at[1, k])
-        cp.start()
-        cld.append(cp)
+        pltpu.make_async_copy(sb_hbm.at[:, pl.ds(cols, 1024)], sb.at[o], sbsem).start()
+    cld = pltpu.make_async_copy(load_hbm, ld, ldsem)
+    cld.start()
 
     cell = tcell_ref[...]
     chosen_xy = onehot((cell >> 7) == iota((64, 1024), 0))
@@ -126,16 +118,15 @@
     for k in range(GROUPS):
         cin[k].wait()
 
-        @pl.loop(k * UNITS // STEP, (k + 1) * UNITS // STEP)
+        @pl.loop(k * STEPS, (k + 1) * STEPS)
         def _(i):
-            for j in range(STEP):
-                u = i * STEP + j
-                a = v0[pl.ds(pl.multiple_of(u * 512, 512), 256), :] * m4[...]
-                bb = v0[pl.ds(pl.multiple_of(u * 512 + 256, 256), 256), :] * m4[...]
-                t = mm(jnp.concatenate([a, bb], axis=1), gg[...]).astype(BF) * ymask[...]
-                t = mm(rmat[...], t)
-                cbuf[pl.ds(pl.multiple_of(u * 64, 64), 32), :] = t[:, :128]
-                cbuf[pl.ds(pl.multiple_of(u * 64 + 32, 32), 32), :] = t[:, 128:]
+            a = [v0[pl.ds(pl.multiple_of(i * 1024 + n * 256, 256), 256), :] * m4[...] for n in range(4)]
+            a = [jnp.concatenate(a[:2], axis=1), jnp.concatenate(a[2:], axis=1)]
+            t = mm(jnp.concatenate(a, axis=0), gg[...]).astype(BF)
+            for n in range(2):
+                c = mm(rmat[...], t[n * 256:(n + 1) * 256, :] * ymask[...])
+                cbuf[pl.ds(pl.multiple_of(i * 128 + n * 64, 64), 32), :] = c[:, :128]
+                cbuf[pl.ds(pl.multiple_of(i * 128 + n * 64 + 32, 32), 32), :] = c[:, 128:]
 
     for x in range(8):
         c2[:, x * 128:(x + 1) * 128] = cbuf[pl.ds(x, 128, stride=8), :].astype(BF)
@@ -144,16 +135,17 @@
 
     pl.semaphore_wait(barrier, peers)
 
-    to_right = [rcopy(tr.at[r, h], tr.at[r, h], ts_s.at[0, h], ts_r.at[0, h], {"row": right}) for h in range(2)]
-    to_left = [rcopy(tr.at[r, h], tr.at[r, h], ts_s.at[1, h], ts_r.at[1, h], {"row": left}) for h in range(2)]
-    from_left = [rcopy(tr.at[left, h], tr.at[left, h], ts_s.at[0, h], ts_r.at[0, h], {"row": right}) for h in range(2)]
-    from_right = [rcopy(tr.at[right, h], tr.at[right, h], ts_s.at[1, h], ts_r.at[1, h], {"row": left}) for h in range(2)]
-    relay_right = rcopy(tr.at[left, 0], tr.at[left, 0], ts_s.at[2, 0], ts_r.at[2, 0], {"row": right})
-    relay_left = rcopy(tr.at[right, 1], tr.at[right, 1], ts_s.at[2, 1], ts_r.at[2, 1], {"row": left})
-    from_far = [
-        rcopy(tr.at[far, 0], tr.at[far, 0], ts_s.at[2, 0], ts_r.at[2, 0], {"row": right}),
-        rcopy(tr.at[far, 1], tr.at[far, 1], ts_s.at[2, 1], ts_r.at[2, 1], {"row": left}),
-    ]
+    def half(who, h, sem, dev):
+        return rcopy(tr.at[who, h], tr.at[who, h], ts_s, ts_r.at[sem], {"row": dev})
+
+    to_right = [half(r, 0, 0, right), half(r, 1, 2, right)]
+    to_left = [half(r, 0, 2, left), half(r, 1, 1, left)]
+    from_left = half(left, 0, 0, right)
+    from_right = half(right, 1, 1, left)
+    relay_right = half(left, 0, 3, right)
+    relay_left = half(right, 1, 3, left)
+    from_sides = rcopy(tr.at[far], tr.at[far], ts_s, ts_r.at[2], {"row": right})
+    from_far = rcopy(tr.at[far], tr.at[far], ts_s, ts_r.at[3], {"row": right})
     to_right[0].start()
     to_left[1].start()
     to_right[1].start()
@@ -226,10 +218,10 @@
         else:
             rows = pl.ds(pl.multiple_of(k * 8, 8), 8)
             src, dst = zs.at[s, d - 4, rows], zh.at[s, (d ^ 1) - 4, rows]
-        return rcopy(src, dst, hs_s.at[s, d, k], hs_r.at[s, d ^ 1, k], nbid[d])
-
-    def send_halos(s, k):
-        for d in (2, 3, 0, 1, 4, 5):
+        return rcopy(src, dst, hs_s.at[d], hs_r.at[s % 2, d ^ 1, k], nbid[d])
+
+    def send_halos(s, k, dirs=(2, 3, 0, 1, 4, 5)):
+        for d in dirs:
             @pl.when(exists[d])
             def _(d=d):
                 halo(s, d, k).start()
@@ -244,94 +236,92 @@
                 else:
                     rows = pl.ds(pl.multiple_of(k * 8, 8), 8)
                     dst = zh.at[s, d - 4, rows]
-                rcopy(dst, dst, hs_s.at[s, d, k], hs_r.at[s, d, k], nbid[d]).wait_recv()
-
-    def faces(s, u, pairs):
-        for i, pair in enumerate(pairs):
+                rcopy(dst, dst, hs_s.at[d], hs_r.at[s % 2, d, k], nbid[d]).wait_recv()
+
+    def faces(s, i, pairs):
+        for n, pair in enumerate(pairs):
             f = mm(emat[...], pair).astype(BF)
             for j in range(2):
-                rows = pl.ds(pl.multiple_of(u * 64 + i * 32 + j * 16, 16), 16)
+                rows = pl.ds(pl.multiple_of(i * 128 + n * 32 + j * 16, 16), 16)
                 for d in range(4):
                     fs[s, d, rows, :] = f[d * 16:(d + 1) * 16, j * 128:(j + 1) * 128]
             v = jnp.concatenate([pair[:, :128], pair[:, 128:]], axis=0)
             zf = nt(wz[...], v)
             for d in range(2):
-                zs[s, d, pl.ds(2 * u + i, 1), :] = zf[d:d + 1, :]
-
-    def sweep(s, u, vin, vout, more_rows, cols):
-        v = [vin[pl.ds(pl.multiple_of(u * 512 + i * 128, 128), 128), :] for i in range(4)]
+                zs[s, d, pl.ds(4 * i + n, 1), :] = zf[d:d + 1, :]
+
+    def sweep(s, i, vin, vout, more_rows, cols):
+        v = [vin[pl.ds(pl.multiple_of(i * 1024 + n * 128, 128), 128), :] for n in range(8)]
         rid = iota((16, 256), 0)
-        ends = jnp.zeros((16, 256), F32)
-        for i in range(2):
-            for d in range(2):
-                ends = jnp.where(rid == 2 * i + d, zh[s, d, pl.ds(2 * u + i, 1), :], ends)
-        lhs = jnp.concatenate([ends] + more_rows, axis=0).astype(BF)
+        lhs = []
+        for n in range(2):
+            ends = jnp.zeros((16, 256), F32)
+            for j in range(2):
+                for d in range(2):
+                    ends = jnp.where(rid == 2 * j + d, zh[s, d, pl.ds(4 * i + 2 * n + j, 1), :], ends)
+            lhs.append(ends)
+        lhs = jnp.concatenate([jnp.concatenate(lhs, axis=1)] + more_rows, axis=0).astype(BF)
         t = tn(lhs, cols)
-        wide = jnp.concatenate([jnp.concatenate(v[:2], axis=0), jnp.concatenate(v[2:], axis=0)], axis=1)
-        z = mm(wide, ss[...]) + t
+        wide = [
+            jnp.concatenate([jnp.concatenate(v[n:n + 2], axis=0), jnp.concatenate(v[n + 2:n + 4], axis=0)], axis=1)
+            for n in (0, 4)
+        ]
+        z = mm(jnp.concatenate(wide, axis=0), ss[...]) + t
         pairs = []
-        for i in range(2):
+        for n in range(4):
             sides = []
             for j in range(2):
-                rows = pl.ds(pl.multiple_of(u * 64 + i * 32 + j * 16, 16), 16)
-                sides.append(jnp.concatenate([v[2 * i + j]] + [hb[s, d, rows, :] for d in range(4)], axis=0))
+                rows = pl.ds(pl.multiple_of(i * 128 + n * 32 + j * 16, 16), 16)
+                sides.append(jnp.concatenate([v[2 * n + j]] + [hb[s, d, rows, :] for d in range(4)], axis=0))
             xy = mm(ah[...], jnp.concatenate(sides, axis=1))
             new = []
             for j in range(2):
-                rows = pl.ds(pl.multiple_of(u * 512 + (2 * i + j) * 128, 128), 128)
-                acc = xy[:, j * 128:(j + 1) * 128] + z[j * 128:(j + 1) * 128, i * 128:(i + 1) * 128]
+                rows = pl.ds(pl.multiple_of(i * 1024 + (2 * n + j) * 128, 128), 128)
+                top = (n // 2) * 256 + j * 128
+                acc = xy[:, j * 128:(j + 1) * 128] + z[top:top + 128, (n % 2) * 128:(n % 2 + 1) * 128]
                 acc = acc + ld[rows, :].astype(F32)
-                n = (0.2 * v[2 * i + j].astype(F32) + w4[...] * acc).astype(BF)
-                vout[rows, :] = n
-                new.append(n)
+                fresh = (0.2 * v[2 * n + j].astype(F32) + w4[...] * acc).astype(BF)
+                vout[rows, :] = fresh
+                new.append(fresh)
             pairs.append(jnp.concatenate(new, axis=1))
         return pairs
 
-    def spread(u, values, places):
-        pick = onehot(iota((128, 512), 0) == 8 * u + (iota((128, 512), 1) >> 6))
-        m = mm(values, pick)
-        return [m[:, :256] * places, m[:, 256:] * places]
+    def spread(i, values, places):
+        m = mm(values, xall[:, pl.ds(pl.multiple_of(i * 1024, 1024), 1024)])
+        m = [m[:, n * 256:(n + 1) * 256] * places for n in range(4)]
+        return [jnp.concatenate([m[0], m[2]], axis=1), jnp.concatenate([m[1], m[3]], axis=1)]
 
     def sweep1(k):
         wait_halos(0, k)
 
-        @pl.loop(k * UNITS // STEP, (k + 1) * UNITS // STEP)
+        @pl.loop(k * STEPS, (k + 1) * STEPS)
         def _(i):
-            for j in range(STEP):
-                u = i * STEP + j
-                faces(1, u, sweep(0, u, v0, v1, [], uu[...]))
-        send_halos(1, k)
+            faces(1, i, sweep(0, i, v0, v1, [], uu[...]))
 
     for k in range(GROUPS):
-        @pl.loop(k * UNITS // STEP, (k + 1) * UNITS // STEP)
+        @pl.loop(k * STEPS, (k + 1) * STEPS)
         def _(i):
-            for j in range(STEP):
-                u = i * STEP + j
-                v = [v0[pl.ds(pl.multiple_of(u * 512 + n * 128, 128), 128), :] for n in range(4)]
-                faces(0, u, [jnp.concatenate(v[:2], axis=1), jnp.concatenate(v[2:], axis=1)])
-        send_halos(0, k)
-        if k == 1:
-            from_left[0].wait_recv()
-            relay_right.start()
-            from_right[1].wait_recv()
-            relay_left.start()
-
+            v = [v0[pl.ds(pl.multiple_of(i * 1024 + n * 128, 128), 128), :] for n in range(8)]
+            faces(0, i, [jnp.concatenate(v[2 * n:2 * n + 2], axis=1) for n in range(4)])
+        send_halos(0, k, (2, 3, 4, 5))
+    from_left.wait_recv()
+    relay_right.start()
+    from_right.wait_recv()
+    relay_left.start()
     for k in range(GROUPS):
-        cld[k].wait()
+        send_halos(0, k, (0, 1))
+    cld.wait()
+    pltpu.make_async_copy(sb, sb, sbsem).wait()
 
     def product(o):
-        csb[o].wait()
         src = (r + o) % 4
         return nt(sb[o, :, 0:512], tr[src, 0]) + nt(sb[o, :, 512:1024], tr[src, 1])
 
     part[...] = product(0)
-    from_left[1].wait_recv()
+    from_sides.wait_recv()
     part[...] += product(3)
-    from_right[0].wait_recv()
     part[...] += product(1)
-    sweep1(0)
-    from_far[0].wait_recv()
-    from_far[1].wait_recv()
+    from_far.wait_recv()
     total = (part[...] + product(2)).reshape(32, 8, 128)
     low, high = total[:, 0:4, :], total[:, 4:8, :]
     first = b == 0
@@ -339,29 +329,32 @@
     csend[...] = jnp.where(first, high, low)
     core = rcopy(csend, crecv, c_s, c_r, {"gz": g + 1 - 2 * b})
     core.start()
-    sweep1(1)
+
+    @pl.loop(0, 8)
+    def _(k):
+        at = k * 1024 + iota((128, 1024), 1)
+        xall[:, pl.ds(pl.multiple_of(k * 1024, 1024), 1024)] = onehot(iota((128, 1024), 0) == (at >> 6))
+
     core.wait_recv()
     qbuf[...] = cown[...] + crecv[...]
     yrecv[y] = qbuf[pl.ds(y * 8, 8)]
-    ycopies = []
     for o in range(1, 4):
         peer = (y + o) % 4
-        cp = rcopy(qbuf.at[pl.ds(peer * 8, 8)], yrecv.at[y], y_s.at[o - 1], y_r.at[o - 1], {"col": peer * 4 + zl})
+        cp = rcopy(qbuf.at[pl.ds(peer * 8, 8)], yrecv.at[y], y_s, y_r, {"col": peer * 4 + zl})
         cp.start()
-        ycopies.append(cp)
-    sweep1(2)
-    for o in range(1, 4):
-        peer = (y + 4 - o) % 4
-        rcopy(yrecv.at[peer], yrecv.at[peer], y_s.at[o - 1], y_r.at[o - 1], {"col": peer * 4 + zl}).wait_recv()
+    sweep1(0)
+    send_halos(1, 0)
+    three = pl.ds(0, 24)
+    yall = rcopy(qbuf.at[three], qbuf.at[three], y_s, y_r, {"col": ((y + 1) % 4) * 4 + zl})
+    yall.wait_recv()
     zsend[...] = (yrecv[0] + yrecv[1]) + (yrecv[2] + yrecv[3])
     zrecv[jz] = zsend[jz]
-    zcopies = []
     for o in range(1, 8):
         peer = (jz + o) % 8
-        cp = rcopy(zsend.at[peer], zrecv.at[jz], z_s.at[o - 1], z_r.at[o - 1], zdev(o))
+        cp = rcopy(zsend.at[peer], zrecv.at[jz], z_s, z_r, zdev(o))
         cp.start()
-        zcopies.append(cp)
-    sweep1(3)
+    sweep1(1)
+    send_halos(1, 1)
 
     for d in range(6):
         @pl.when(exists[d])
@@ -396,9 +389,10 @@
     zcols[0:16, :] = uu[...].astype(F32)
     zcols3[0:16, :] = uu[...].astype(F32)
 
-    for o in range(1, 8):
-        peer = (jz + 8 - o) % 8
-        rcopy(zrecv.at[peer], zrecv.at[peer], z_s.at[o - 1], z_r.at[o - 1], zdev(8 - o)).wait_recv()
+    sweep1(2)
+    seven = pl.ds(0, 7)
+    zall = rcopy(zsend.at[seven], zrecv.at[seven], z_s, z_r, zdev(1))
+    zall.wait_recv()
     own = zrecv[0]
     for j in range(1, 8):
         own = own + zrecv[j]
@@ -411,11 +405,12 @@
         def _(d=d):
             rcopy(gbuf, gnb.at[d ^ 1], g_s.at[d], g_r.at[d ^ 1], nbid[d]).start()
     fall[g] = own
-    fcopies = []
     for o in range(1, 4):
-        cp = rcopy(fbuf, fall.at[g], f_s.at[o - 1], f_r.at[o - 1], {"gz": (g + o) % 4})
+        cp = rcopy(fbuf, fall.at[g], f_s, f_r, {"gz": (g + o) % 4})
         cp.start()
-        fcopies.append(cp)
+    send_halos(1, 2)
+    sweep1(3)
+    send_halos(1, 3)
 
     for d in range(6):
         @pl.when(exists[d])
@@ -437,50 +432,45 @@
     def _(k):
         wait_halos(1, k)
 
-        @pl.loop(k * UNITS // STEP, (k + 1) * UNITS // STEP)
+        @pl.loop(k * STEPS, (k + 1) * STEPS)
         def _(i):
-            for j in range(STEP):
-                u = i * STEP + j
-                rows = spread(u, val[...].astype(BF), lmask[...])
-                faces(2, u, sweep(1, u, v1, v2, rows, zcols[...].astype(BF)))
+            rows = spread(i, val[...].astype(BF), lmask[...])
+            faces(2, i, sweep(1, i, v1, v2, rows, zcols[...].astype(BF)))
         send_halos(2, k)
 
     def put(k):
         rows = pl.ds(pl.multiple_of(k * 2048, 2048), 2048)
-        return pltpu.make_async_copy(v3.at[rows], out_hbm.at[rows], outsem.at[k])
+        return pltpu.make_async_copy(v3.at[rows], out_hbm.at[rows], outsem)
 
     @pl.loop(0, GROUPS)
     def _(k):
         wait_halos(2, k)
 
-        @pl.loop(k * UNITS // STEP, (k + 1) * UNITS // STEP)
+        @pl.loop(k * STEPS, (k + 1) * STEPS)
         def _(i):
-            for j in range(STEP):
-                u = i * STEP + j
-                rows = spread(u, val3[...].astype(BF), lmask[0:8, :])
-                sweep(2, u, v2, v3, rows, zcols3[...].astype(BF))
+            rows = spread(i, val3[...].astype(BF), lmask[0:8, :])
+            sweep(2, i, v2, v3, rows, zcols3[...].astype(BF))
         put(k).start()
 
-    for o in range(1, 4):
-        peer = (g + 4 - o) % 4
-        rcopy(fall.at[peer], fall.at[peer], f_s.at[o - 1], f_r.at[o - 1], {"gz": peer}).wait_recv()
+    others = pl.ds(0, 3)
+    fgot = rcopy(zsend.at[others], fall.at[others], f_s, f_r, {"gz": (g + 1) % 4})
+    fgot.wait_recv()
     sel = jnp.where(iota((32, 128), 1) == g * 32 + iota((32, 128), 0), 1.0, 0.0)
     rows16 = jnp.concatenate([fall[0], fall[1], fall[2], fall[3]], axis=0)
-    flux_ref[...] = nt(sel, rows16, precision=lax.Precision.HIGHEST)
-
-    for cp in to_right + to_left + [relay_right, relay_left, core] + ycopies + zcopies + fcopies:
+    flux_ref[...] = nt(rows16, sel, precision=lax.Precision.HIGHEST)
+
+    sent = pl.ds(0, 3)
+    rcopy(tr.at[sent], tr.at[sent], ts_s, ts_r.at[0], {"row": right}).wait_send()
+    for cp in (core, yall, zall, fgot):
         cp.wait_send()
     for d in range(6):
         @pl.when(exists[d])
         def _(d=d):
             rcopy(cinfo, cnb.at[d ^ 1], i_s.at[d], i_r.at[d ^ 1], nbid[d]).wait_send()
             rcopy(gbuf, gnb.at[d ^ 1], g_s.at[d], g_r.at[d ^ 1], nbid[d]).wait_send()
-            for s in range(3):
-                @pl.loop(0, GROUPS)
-                def _(k):
-                    halo(s, d, k).wait_send()
-    for k in range(GROUPS):
-        put(k).wait()
+            sent = fs.at[:, d] if d < 4 else zs.at[:, d - 4]
+            rcopy(sent, sent, hs_s.at[d], hs_r.at[0, d, 0], nbid[d]).wait_send()
+    pltpu.make_async_copy(v3, out_hbm, outsem).wait()
 
 
 def per_device(volume_field, volume_load, coefficient, surface_block, trace_cell, flux_cell):
@@ -495,21 +485,20 @@
         vm((128, 192), BF), vm((64, 128), BF), vm((256, 256), BF), vm((256, 256), BF),
         vm((32, 256), BF), vm((16, 128), BF), vm((16, 256), BF), vm((256, 128), BF), vm((256, 256), BF),
         vm((1024, 128), F32), vm((128, 1024), BF),
-        vm((1024, 1024), BF),
+        vm((1024, 1024), BF), vm((128, 8192), BF),
         vm((256, 128), F32), vm((32, 4, 128), F32), vm((32, 4, 128), F32), vm((32, 4, 128), F32),
         vm((32, 4, 128), F32), vm((4, 8, 4, 128), F32), vm((8, 4, 128), F32), vm((8, 4, 128), F32),
         vm((4, 128), F32), vm((4, 4, 128), F32),
         vm((8, 128), F32), vm((6, 8, 128), F32), vm((8, 128), F32), vm((6, 8, 128), F32),
         vm((56, 256), F32), vm((128, 256), F32), vm((32, 256), F32), vm((56, 128), F32), vm((8, 128), F32),
-        dma((2, GROUPS)), dma((4,)), dma((GROUPS,)), dma((3, 6, GROUPS)), dma((3, 6, GROUPS)),
-        dma((3, 2)), dma((3, 2)), dma, dma, dma((3,)), dma((3,)), dma((7,)), dma((7,)),
-        dma((3,)), dma((3,)), dma((6,)), dma((6,)), dma((6,)), dma((6,)),
+        dma((GROUPS,)), dma, dma, dma, dma((6,)), dma((2, 6, GROUPS)),
+        dma, dma((4,)), dma, dma, dma, dma, dma, dma, dma, dma, dma((6,)), dma((6,)), dma((6,)), dma((6,)),
     ]
     anywhere = pl.BlockSpec(memory_space=pl.ANY)
     local = pl.BlockSpec(memory_space=pltpu.VMEM)
     new_field, surface_flux = pl.pallas_call(
         kernel,
-        out_shape=(jax.ShapeDtypeStruct((rows, 128), BF), jax.ShapeDtypeStruct((32, 16), F32)),
+        out_shape=(jax.ShapeDtypeStruct((rows, 128), BF), jax.ShapeDtypeStruct((16, 32), F32)),
         in_specs=[anywhere, anywhere, local, anywhere, local, pl.BlockSpec(memory_space=pltpu.SMEM)],
         out_specs=(anywhere, local),
         scratch_shapes=scratch,
@@ -524,7 +513,7 @@
         trace_cell.reshape(1, 1024),
         flux_cell.reshape(4),
     )
-    return new_field.reshape(volume_field.shape), surface_flux
+    return new_field.reshape(volume_field.shape), surface_flux.T
 
 
 def solution(mesh):

time: 69.4 us -> 61.9 us (0.89)
  the two profiles are of different devices: /device:TPU:24 before, /device:TPU:11 now
where the time goes in v3:
time: 61.9 us; the launch traced here: 61.8 us
  Pallas kernels  57.4 us (93%)
  local copies, waits for them, and re-layouts  3.69 us (6%)
  between operations  0.65 us (1%)
    pallas_call x1, Pallas kernels, per_device(): pl.pallas_call(kernel, out_shape=(jax.ShapeDtypeStruct((rows, 128), BF),...  57.4 us
    unnamed x4, local copies, waits for them, and re-layouts  3.69 us

profile of v3, /device:TPU:11, one launch (start us, length us, event | category | flops | bytes accessed | tf_op | source)
XLA Modules:
  0.0 61.8 jit_solution(9999517769705403586)
XLA Ops:
  0.6 57.4 %shard_map.77 = (bf16[8192,128]{1,0:T(8,128)(2,1)}, f32[16,32]{1,0:T(8,128)}) custom-call(bf16[8192,128]{1,0:T(8,128)(2,1)} %bitcast.8, bf16[8192,128]{1,0:T(8,128)(2,1)} %bitcast.9, f32[64,128]{1,0:T(8,128)} %bitcast.10, bf16[256,16384]{1,0:T(8,128)(2,1)} %sb_hbm.1, s32[1,1024]{1,0:T(1,128)} %bitcast.12, s32[4]{0:T(128)} %bitcast.13), custom_call_target="tpu_custom_call" | custom-call | tf_op jit(solution)/shard_map/pallas_call | solution.py:499
  58.1 0.0 copy-start
  58.1 3.1 %copy.10 = bf16[128,8,8,128]{3,2,1,0:T(8,128)(2,1)} copy(bf16[128,8,8,128]{3,2,1,0:T(8,128)(2,1)} %bitcast.7) | data formatting | bytes 4194304
  61.2 0.0 copy-done
  61.2 0.6 copy.11
Async XLA Ops:
  58.1 3.1 %copy-start = (f32[16,32]{1,0:T(8,128)S(1)}, f32[16,32]{1,0:T(8,128)}, u32[]{:S(2)}) copy-start(f32[16,32]{1,0:T(8,128)} %get-tuple-element.5) | copy-start | bytes 6148

commit v4 on v3

v4 whole, which is shorter than its diff:
```python
import functools

import jax
import jax.numpy as jnp
from jax import lax
from jax.experimental import pallas as pl
from jax.experimental.pallas import tpu as pltpu
from jax.sharding import PartitionSpec as P

MESH = pl.DeviceIdType.MESH
BF = jnp.bfloat16
F32 = jnp.float32
I32 = jnp.int32
OMEGA = 0.8
GROUPS = 8
OFFS = ((-1, 0, 0), (1, 0, 0), (0, -1, 0), (0, 1, 0), (0, 0, -1), (0, 0, 1))


def iota(shape, dim):
    return lax.broadcasted_iota(I32, shape, dim)


def onehot(cond):
    return jnp.where(cond, 1.0, 0.0).astype(BF)


def nt(a, b, **kw):
    return lax.dot_general(a, b, (((1,), (1,)), ((), ())), preferred_element_type=F32, **kw)


def tn(a, b):
    return lax.dot_general(a, b, (((0,), (0,)), ((), ())), preferred_element_type=F32)


def mm(a, b):
    return jnp.dot(a, b, preferred_element_type=F32)


def kernel(
    field_hbm, load_hbm, coef_ref, sb_hbm, tcell_ref, fcell_ref,
    out_hbm, flux_ref,
    v0, ld, v1, v2, v3, sb, tr, w4, hb, fs, zh, zs,
    ah, emat, ss, gg, wz, uu, m4, picked, cbuf, c2, pbuf, xall,
    part, cown, csend, crecv, qbuf, zrecv, fbuf, fall,
    gbuf, gnb, cinfo, cnb, lmask, zcols, zcols3, val, val3,
    insem, ldsem, sbsem, outsem, hs_s, hs_r, ts_s, ts_r, c_s, c_r, z_s, z_r, round_sem,
    f_s, f_r, g_s, g_r, i_s, i_r,
):
    r = lax.axis_index("row")
    c = lax.axis_index("col")
    g = lax.axis_index("gz")
    y, zl = c // 4, c % 4
    zhi, b = g // 2, g % 2
    right, left, far = (r + 1) % 4, (r + 3) % 4, (r + 2) % 4
    me = c * 2 + zhi

    exists = (r > 0, r < 3, c > 0, c < 15, g > 0, g < 3)
    nbid = ({"row": r - 1}, {"row": r + 1}, {"col": c - 1}, {"col": c + 1}, {"gz": g - 1}, {"gz": g + 1})

    def rcopy(src, dst, ss, rs, dev):
        return pltpu.make_async_remote_copy(
            src_ref=src, dst_ref=dst, send_sem=ss, recv_sem=rs, device_id=dev, device_id_type=MESH
        )

    barrier = pltpu.get_barrier_semaphore()

    def greet(dev):
        pl.semaphore_signal(barrier, inc=1, device_id=dev, device_id_type=MESH)

    def holder(j):
        return {"col": j // 2, "gz": (j % 2) * 2 + b}

    jz = zl * 2 + zhi
    ypeers = [{"col": ((y + o) % 4) * 4 + zl} for o in range(1, 4)]
    for o in range(1, 4):
        greet({"row": (r + o) % 4})
    for dev in ypeers:
        greet(dev)
    for o in range(1, 8):
        j = (jz + o) % 8
        greet({"col": y * 4 + j // 2, "gz": (j % 2) * 2 + b})
    greet({"gz": zhi * 2 + 1 - b})
    greet({"gz": (1 - zhi) * 2 + 1 - b})
    wraps = ((zl == 0) & (c > 0), (zl == 3) & (c < 15))
    for d in range(2):
        @pl.when(wraps[d])
        def _(d=d):
            greet(nbid[2 + d])
    peers = 15 + jnp.where(wraps[0], 1, 0) + jnp.where(wraps[1], 1, 0)

    cin = []
    for k in range(4):
        rows = pl.ds(k * 2048, 2048)
        cp = pltpu.make_async_copy(field_hbm.at[rows], v0.at[rows], insem.at[k])
        cp.start()
        cin.append(cp)

    cell = tcell_ref[...]
    chosen_xy = onehot((cell >> 7) == iota((64, 1024), 0))
    chosen_z = onehot((cell & 127) == iota((128, 1024), 0))
    mask = nt(chosen_xy, chosen_z).astype(BF)
    for k in range(4):
        m4[k * 64:(k + 1) * 64, :] = mask
    for n in range(8):
        lane = iota((128, 128), 1) - n * 16
        gg[n * 128:(n + 1) * 128, :] = onehot(lane == (iota((128, 128), 0) >> 3))

    @pl.loop(0, 8)
    def _(k):
        rows = pl.ds(pl.multiple_of(k * 128, 128), 128)
        pbuf[rows, :] = onehot((cell >> 3) == iota((128, 1024), 0) + k * 128)

    for k in range(4):
        cin[k].wait()

        @pl.loop(0, 2)
        def _(i, k=k):
            for n in range(4):
                rows = pl.ds(pl.multiple_of(k * 2048 + i * 1024 + n * 256, 256), 256)
                picked[rows, :] = (v0[rows, :] * m4[...]).astype(F32)

        lanes = [picked[pl.ds(k * 2048 + n, 256, stride=8), :].astype(BF) for n in range(8)]
        cbuf[k * 256:(k + 1) * 256, :] = mm(jnp.concatenate(lanes, axis=1), gg[...])

    for o in range(4):
        cols = pl.multiple_of((((r + o) % 4) * 4 + g) * 1024, 1024)
        pltpu.make_async_copy(sb_hbm.at[:, pl.ds(cols, 1024)], sb.at[o], sbsem).start()
    cld = pltpu.make_async_copy(load_hbm, ld, ldsem)
    cld.start()

    for x in range(8):
        c2[:, x * 128:(x + 1) * 128] = cbuf[pl.ds(x, 128, stride=8), :].astype(BF)
    for h in range(2):
        tr[r, h] = mm(c2[...], pbuf[:, h * 512:(h + 1) * 512]).astype(BF)

    pl.semaphore_wait(barrier, peers)

    def half(who, h, sem, dev):
        return rcopy(tr.at[who, h], tr.at[who, h], ts_s, ts_r.at[sem], {"row": dev})

    to_right = [half(r, 0, 0, right), half(r, 1, 2, right)]
    to_left = [half(r, 0, 2, left), half(r, 1, 1, left)]
    from_left = half(left, 0, 0, right)
    from_right = half(right, 1, 1, left)
    relay_right = half(left, 0, 3, right)
    relay_left = half(right, 1, 3, left)
    from_sides = rcopy(tr.at[far], tr.at[far], ts_s, ts_r.at[2], {"row": right})
    from_far = rcopy(tr.at[far], tr.at[far], ts_s, ts_r.at[3], {"row": right})
    to_right[0].start()
    to_left[1].start()
    to_right[1].start()
    to_left[0].start()
    for dev in ypeers:
        pl.semaphore_signal(round_sem, inc=1, device_id=dev, device_id_type=MESH)

    p, q = iota((64, 128), 0), iota((64, 128), 1)
    d, o = p >> 4, p & 7
    qx, qy = (q >> 3) & 7, q & 7
    hit = jnp.where(
        d < 2,
        jnp.where(qx == d * 7, jnp.where(qy == o, 1.0, 0.0), 0.0),
        jnp.where(qy == (d - 2) * 7, jnp.where(qx == o, 1.0, 0.0), 0.0),
    )
    emat[...] = jnp.where(((p >> 3) & 1) == (q >> 6), hit, 0.0).astype(BF)
    wz[...] = onehot(iota((16, 128), 1) == jnp.where(iota((16, 128), 0) < 2, iota((16, 128), 0) * 127, -1))

    def halo(s, d, k):
        if d < 4:
            rows = pl.ds(pl.multiple_of(k * 128, 128), 128)
            src, dst = fs.at[s, d, rows], hb.at[s, d ^ 1, rows]
        else:
            src, dst = zs.at[s, d - 4, k], zh.at[s, (d ^ 1) - 4, k]
        return rcopy(src, dst, hs_s.at[d], hs_r.at[s % 2, d // 2, k], nbid[d])

    def send_halos(s, k, dirs=(2, 3, 0, 1, 4, 5)):
        for d in dirs:
            @pl.when(exists[d])
            def _(d=d):
                halo(s, d, k).start()

    def wait_halos(s, k):
        for axis in range(3):
            low, high = exists[2 * axis], exists[2 * axis + 1]

            def arrived(first, count, axis=axis):
                sides = pl.ds(first, count)
                if axis < 2:
                    dst = hb.at[s, sides, pl.ds(pl.multiple_of(k * 128, 128), 128)]
                else:
                    dst = zh.at[s, sides, k]
                rcopy(dst, dst, hs_s.at[0], hs_r.at[s % 2, axis, k], {"row": right}).wait_recv()
            base = 2 * axis if axis < 2 else 0

            @pl.when(low & high)
            def _(arrived=arrived, base=base):
                arrived(base, 2)

            @pl.when(low & jnp.logical_not(high))
            def _(arrived=arrived, base=base):
                arrived(base, 1)

            @pl.when(high & jnp.logical_not(low))
            def _(arrived=arrived, base=base):
                arrived(base + 1, 1)

    def faces(s, i, pairs):
        for n, pair in enumerate(pairs):
            f = mm(emat[...], pair).astype(BF)
            for j in range(2):
                rows = pl.ds(pl.multiple_of(i * 128 + n * 32 + j * 16, 16), 16)
                for d in range(4):
                    fs[s, d, rows, :] = f[d * 16:(d + 1) * 16, j * 128:(j + 1) * 128]
            v = jnp.concatenate([pair[:, :128], pair[:, 128:]], axis=0)
            zf = nt(wz[...], v)
            for d in range(2):
                zs[s, d, i, n:n + 1, :] = zf[d:d + 1, :]

    def sweep(s, i, vin, vout, more_rows, cols):
        v = [vin[pl.ds(pl.multiple_of(i * 1024 + n * 128, 128), 128), :] for n in range(8)]
        rid = iota((16, 256), 0)
        lhs = []
        for n in range(2):
            ends = jnp.zeros((16, 256), F32)
            for j in range(2):
                for d in range(2):
                    ends = jnp.where(rid == 2 * j + d, zh[s, d, i, 2 * n + j:2 * n + j + 1, :], ends)
            lhs.append(ends)
        lhs = jnp.concatenate([jnp.concatenate(lhs, axis=1)] + more_rows, axis=0).astype(BF)
        t = tn(lhs, cols)
        wide = [
            jnp.concatenate([jnp.concatenate(v[n:n + 2], axis=0), jnp.concatenate(v[n + 2:n + 4], axis=0)], axis=1)
            for n in (0, 4)
        ]
        z = mm(jnp.concatenate(wide, axis=0), ss[...]) + t
        pairs = []
        for n in range(4):
            sides = []
            for j in range(2):
                rows = pl.ds(pl.multiple_of(i * 128 + n * 32 + j * 16, 16), 16)
                sides.append(jnp.concatenate([v[2 * n + j]] + [hb[s, d, rows, :] for d in range(4)], axis=0))
            xy = mm(ah[...], jnp.concatenate(sides, axis=1))
            new = []
            for j in range(2):
                rows = pl.ds(pl.multiple_of(i * 1024 + (2 * n + j) * 128, 128), 128)
                top = (n // 2) * 256 + j * 128
                acc = xy[:, j * 128:(j + 1) * 128] + z[top:top + 128, (n % 2) * 128:(n % 2 + 1) * 128]
                acc = acc + ld[rows, :].astype(F32)
                fresh = (0.2 * v[2 * n + j].astype(F32) + w4[...] * acc).astype(BF)
                vout[rows, :] = fresh
                new.append(fresh)
            pairs.append(jnp.concatenate(new, axis=1))
        return pairs

    def spread(i, values, places):
        m = mm(values, xall[:, pl.ds(pl.multiple_of(i * 1024, 1024), 1024)])
        m = [m[:, n * 256:(n + 1) * 256] * places for n in range(4)]
        return [jnp.concatenate([m[0], m[2]], axis=1), jnp.concatenate([m[1], m[3]], axis=1)]

    def sweep1(first, last):
        @pl.loop(first, last)
        def _(k):
            wait_halos(0, k)
            faces(1, k, sweep(0, k, v0, v1, [], uu[...]))
            send_halos(1, k)

    @pl.loop(0, GROUPS)
    def _(k):
        v = [v0[pl.ds(pl.multiple_of(k * 1024 + n * 128, 128), 128), :] for n in range(8)]
        faces(0, k, [jnp.concatenate(v[2 * n:2 * n + 2], axis=1) for n in range(4)])
        send_halos(0, k, (2, 3, 4, 5))

    p, q = iota((128, 256), 0), iota((128, 256), 1)
    px, py = (p >> 3) & 7, p & 7
    dx = jnp.abs(px - ((q >> 3) & 7))
    dy = jnp.abs(py - (q & 7))
    inside = jnp.where((p >> 6) == ((q >> 6) & 1), jnp.where(dx + dy == 1, 1.0, 0.0), 0.0)
    d, o = (q >> 4) & 7, q & 7
    hit = jnp.where(
        d < 2,
        jnp.where(px == d * 7, jnp.where(py == o, 1.0, 0.0), 0.0),
        jnp.where(py == (d - 2) * 7, jnp.where(px == o, 1.0, 0.0), 0.0),
    )
    hit = jnp.where(((q >> 3) & 1) == (p >> 6), hit, 0.0)
    ah[...] = jnp.where(q < 128, inside, hit)[:, :192].astype(BF)
    p, q = iota((256, 256), 0), iota((256, 256), 1)
    ss[...] = jnp.where((p >> 7) == (q >> 7), jnp.where(jnp.abs(p - q) == 1, 1.0, 0.0), 0.0).astype(BF)
    p, q = iota((16, 256), 0), iota((16, 256), 1)
    uu[...] = jnp.where(p < 4, jnp.where(q == (p >> 1) * 128 + (p & 1) * 127, 1.0, 0.0), 0.0).astype(BF)

    w = OMEGA / (6.0 + coef_ref[...])
    for k in range(2):
        w4[k * 64:(k + 1) * 64, :] = w

    row8 = iota((8, 128), 0) & 3
    cells = jnp.zeros((8, 128), I32)
    weight = jnp.zeros((8, 128), F32)
    number = iota((64, 128), 0) * 128 + iota((64, 128), 1)
    for k in range(4):
        fc = fcell_ref[k]
        wk = jnp.sum(jnp.where(number == fc, w, 0.0), axis=(0, 1), keepdims=True)
        cells = jnp.where(row8 == k, fc, cells)
        weight = jnp.where(row8 == k, wk, weight)
    cinfo[...] = cells.astype(F32)
    for d in range(6):
        @pl.when(exists[d])
        def _(d=d):
            rcopy(cinfo, cnb.at[d ^ 1], i_s.at[d], i_r.at[d ^ 1], nbid[d]).start()

    for d in range(6):
        @pl.when(jnp.logical_not(exists[d]))
        def _(d=d):
            cnb[d] = jnp.zeros((8, 128), F32)
            gnb[d] = jnp.zeros((8, 128), F32)
            for s in range(3):
                if d < 4:
                    @pl.loop(0, 8)
                    def _(k, s=s):
                        hb[s, d, pl.ds(pl.multiple_of(k * 128, 128), 128), :] = jnp.zeros((128, 128), BF)
                else:
                    zh[s, d - 4] = jnp.zeros((GROUPS, 4, 256), F32)

    @pl.loop(0, 8)
    def _(k):
        at = k * 1024 + iota((128, 1024), 1)
        xall[:, pl.ds(pl.multiple_of(k * 1024, 1024), 1024)] = onehot(iota((128, 1024), 0) == (at >> 6))

    from_left.wait_recv()
    relay_right.start()
    from_right.wait_recv()
    relay_left.start()

    @pl.loop(0, GROUPS)
    def _(k):
        send_halos(0, k, (0, 1))

    cld.wait()
    pltpu.make_async_copy(sb, sb, sbsem).wait()

    def product(o):
        src = (r + o) % 4
        return nt(sb[o, :, 0:512], tr[src, 0]) + nt(sb[o, :, 512:1024], tr[src, 1])

    part[...] = product(0)
    from_sides.wait_recv()
    part[...] += product(3)
    part[...] += product(1)
    from_far.wait_recv()
    total = (part[...] + product(2)).reshape(32, 8, 128)
    low, high = total[:, 0:4, :], total[:, 4:8, :]
    first = b == 0
    cown[...] = jnp.where(first, low, high)
    csend[...] = jnp.where(first, high, low)
    core = rcopy(csend, crecv, c_s, c_r, {"gz": g + 1 - 2 * b})
    core.start()
    sweep1(0, 1)

    core.wait_recv()
    qbuf[...] = cown[...] + crecv[...]
    pl.semaphore_wait(round_sem, 3)
    zrecv[me] = qbuf[me]

    @pl.loop(1, 32)
    def _(o):
        j = (me + o) % 32
        rcopy(qbuf.at[j], zrecv.at[me], z_s, z_r, holder(j)).start()
    sweep1(1, 4)

    for d in range(6):
        @pl.when(exists[d])
        def _(d=d):
            rcopy(cnb.at[d], cnb.at[d], i_s.at[d], i_r.at[d], nbid[d]).wait_recv()
    mine = iota((8, 128), 0) < 4
    lane = iota((8, 256), 1) & 63
    for k in range(7):
        if k == 0:
            tx, ty, tz = cells >> 10, (cells >> 7) & 7, cells & 127
        else:
            ox, oy, oz = OFFS[k - 1]
            other = cnb[k - 1].astype(I32)
            at = jnp.where(mine, cells, other)
            tx = (at >> 10) + jnp.where(mine, ox, 7 * ox)
            ty = ((at >> 7) & 7) + jnp.where(mine, oy, 7 * oy)
            tz = (at & 127) + jnp.where(mine, oz, 127 * oz)
        txy = jnp.where((tx >= 0) & (tx < 8) & (ty >= 0) & (ty < 8), tx * 8 + ty, -1)
        tz = jnp.where((tz >= 0) & (tz < 128), tz, -1)
        spots = jnp.where(jnp.concatenate([txy, txy], axis=1) == lane, 1.0, 0.0)
        cols = jnp.where(tz == iota((8, 128), 1), 1.0, 0.0)
        lmask[k * 8:k * 8 + 8, :] = spots
        zcols[16 + k * 8:24 + k * 8, 0:128] = cols
        zcols[16 + k * 8:24 + k * 8, 128:256] = jnp.zeros((8, 128), F32)
        zcols[72 + k * 8:80 + k * 8, 0:128] = jnp.zeros((8, 128), F32)
        zcols[72 + k * 8:80 + k * 8, 128:256] = cols
        if k == 0:
            zcols3[16:24, 0:128] = cols
            zcols3[16:24, 128:256] = jnp.zeros((8, 128), F32)
            zcols3[24:32, 0:128] = jnp.zeros((8, 128), F32)
            zcols3[24:32, 128:256] = cols
    zcols[0:16, :] = uu[...].astype(F32)
    zcols3[0:16, :] = uu[...].astype(F32)

    most = pl.ds(0, 31)
    zall = rcopy(qbuf.at[most], zrecv.at[most], z_s, z_r, holder((me + 1) % 32))
    zall.wait_recv()
    own = jnp.sum(zrecv[...], axis=0)
    fbuf[...] = own
    own8 = jnp.concatenate([own, own], axis=0)
    gvals = weight * own8
    gbuf[...] = gvals
    for d in range(6):
        @pl.when(exists[d])
        def _(d=d):
            rcopy(gbuf, gnb.at[d ^ 1], g_s.at[d], g_r.at[d ^ 1], nbid[d]).start()
    fall[g] = own
    for o in range(1, 4):
        cp = rcopy(fbuf, fall.at[g], f_s, f_r, {"gz": (g + o) % 4})
        cp.start()
    sweep1(4, 8)

    for d in range(6):
        @pl.when(exists[d])
        def _(d=d):
            rcopy(gnb.at[d], gnb.at[d], g_s.at[d], g_r.at[d], nbid[d]).wait_recv()

    def split(values):
        hi = values.astype(BF).astype(F32)
        return hi, values - hi

    hi, lo = split(1.2 * own8)
    val[0:8, :] = jnp.where(mine, hi, lo)
    for d in range(6):
        val[8 + d * 8:16 + d * 8, :] = jnp.where(mine, gvals, gnb[d])
    hi, lo = split(own8)
    val3[...] = jnp.where(mine, hi, lo)

    @pl.loop(0, GROUPS)
    def _(k):
        wait_halos(1, k)
        rows = spread(k, val[...].astype(BF), lmask[...])
        faces(2, k, sweep(1, k, v1, v2, rows, zcols[...].astype(BF)))
        send_halos(2, k)

    def put(k):
        rows = pl.ds(pl.multiple_of(k * 1024, 1024), 1024)
        return pltpu.make_async_copy(v3.at[rows], out_hbm.at[rows], outsem)

    @pl.loop(0, GROUPS)
    def _(k):
        wait_halos(2, k)
        rows = spread(k, val3[...].astype(BF), lmask[0:8, :])
        sweep(2, k, v2, v3, rows, zcols3[...].astype(BF))
        put(k).start()

    others = pl.ds(0, 3)
    fgot = rcopy(qbuf.at[others], fall.at[others], f_s, f_r, {"gz": (g + 1) % 4})
    fgot.wait_recv()
    sel = jnp.where(iota((32, 128), 1) == g * 32 + iota((32, 128), 0), 1.0, 0.0)
    rows16 = jnp.concatenate([fall[0], fall[1], fall[2], fall[3]], axis=0)
    flux_ref[...] = nt(rows16, sel, precision=lax.Precision.HIGHEST)

    sent = pl.ds(0, 3)
    rcopy(tr.at[sent], tr.at[sent], ts_s, ts_r.at[0], {"row": right}).wait_send()
    for cp in (core, zall, fgot):
        cp.wait_send()
    for d in range(6):
        @pl.when(exists[d])
        def _(d=d):
            rcopy(cinfo, cnb.at[d ^ 1], i_s.at[d], i_r.at[d ^ 1], nbid[d]).wait_send()
            rcopy(gbuf, gnb.at[d ^ 1], g_s.at[d], g_r.at[d ^ 1], nbid[d]).wait_send()
            sent = fs.at[:, d] if d < 4 else zs.at[:, d - 4]
            rcopy(sent, sent, hs_s.at[d], hs_r.at[0, d // 2, 0], nbid[d]).wait_send()
    pltpu.make_async_copy(v3, out_hbm, outsem).wait()


def hand_over(src, dst, held, came, left):
    into = [pltpu.make_async_copy(src.at[pl.ds(k * 1024, 1024)], held.at[k], came.at[k]) for k in range(8)]
    out = [pltpu.make_async_copy(held.at[k], dst.at[pl.ds(k * 1024, 1024)], left.at[k]) for k in range(8)]
    for cp in into:
        cp.start()
    for k in range(8):
        into[k].wait()
        out[k].start()
    for cp in out:
        cp.wait()


def per_device(volume_field, volume_load, coefficient, surface_block, trace_cell, flux_cell):
    side_count, first_span, second_span, third_span = volume_field.shape
    rows = side_count * first_span * second_span
    vm = pltpu.VMEM
    dma = pltpu.SemaphoreType.DMA
    scratch = [
        vm((rows, 128), BF), vm((rows, 128), BF), vm((rows, 128), BF), vm((rows, 128), BF), vm((rows, 128), BF),
        vm((4, 256, 1024), BF), vm((4, 2, 128, 512), BF), vm((128, 128), F32),
        vm((3, 4, 1024, 128), BF), vm((3, 4, 1024, 128), BF), vm((3, 2, GROUPS, 4, 256), F32), vm((3, 2, GROUPS, 4, 256), F32),
        vm((128, 192), BF), vm((64, 128), BF), vm((256, 256), BF), vm((1024, 128), BF),
        vm((16, 128), BF), vm((16, 256), BF), vm((256, 128), BF), vm((rows, 128), F32),
        vm((1024, 128), F32), vm((128, 1024), BF),
        vm((1024, 1024), BF), vm((128, 8192), BF),
        vm((256, 128), F32), vm((32, 4, 128), F32), vm((32, 4, 128), F32), vm((32, 4, 128), F32),
        vm((32, 4, 128), F32), vm((32, 4, 128), F32),
        vm((4, 128), F32), vm((4, 4, 128), F32),
        vm((8, 128), F32), vm((6, 8, 128), F32), vm((8, 128), F32), vm((6, 8, 128), F32),
        vm((56, 256), F32), vm((128, 256), F32), vm((32, 256), F32), vm((56, 128), F32), vm((8, 128), F32),
        dma((4,)), dma, dma, dma, dma((6,)), dma((2, 3, GROUPS)),
        dma, dma((4,)), dma, dma, dma, dma, pltpu.SemaphoreType.REGULAR, dma, dma, dma((6,)), dma((6,)), dma((6,)), dma((6,)),
    ]
    anywhere = pl.BlockSpec(memory_space=pl.ANY)
    outside = pl.BlockSpec(memory_space=pltpu.HBM)
    local = pl.BlockSpec(memory_space=pltpu.VMEM)
    new_field, surface_flux = pl.pallas_call(
        kernel,
        out_shape=(jax.ShapeDtypeStruct((rows, 128), BF), jax.ShapeDtypeStruct((16, 32), F32)),
        in_specs=[outside, outside, local, outside, local, pl.BlockSpec(memory_space=pltpu.SMEM)],
        out_specs=(anywhere, local),
        scratch_shapes=scratch,
        compiler_params=pltpu.CompilerParams(
            collective_id=0, has_side_effects=True, vmem_limit_bytes=60 * 1024 * 1024
        ),
    )(
        volume_field.reshape(rows, 128),
        volume_load.reshape(rows, 128),
        coefficient.reshape(64, 128),
        surface_block,
        trace_cell.reshape(1, 1024),
        flux_cell.reshape(4),
    )
    new_field = pl.pallas_call(
        hand_over,
        out_shape=jax.ShapeDtypeStruct((rows, 128), BF),
        in_specs=[anywhere],
        out_specs=anywhere,
        scratch_shapes=[vm((8, rows // 8, 128), BF), dma((8,)), dma((8,))],
    )(new_field)
    return new_field.reshape(volume_field.shape), surface_flux.T


def solution(mesh):
    in_specs = (
        P(None, "row", "col", "gz"),
        P(None, "row", "col", "gz"),
        P("row", "col", "gz"),
        P("row", "col"),
        P("row", "col", "gz", None),
        P("row", "col", "gz", None),
    )
    out_specs = (P(None, "row", "col", "gz"), P("gz", ("row", "col")))
    return jax.shard_map(
        per_device, mesh=mesh, in_specs=in_specs, out_specs=out_specs, check_vma=False
    )
```

time: 61.9 us -> 57.8 us (0.934)
  local copies, waits for them, and re-layouts: 3.69 us -> 0.61 us
  Pallas kernels: 57.4 us -> 56.3 us
    pallas_call x1, Pallas kernels: 57.4 us -> 53.9 us  [per_device(): pl.pallas_call(kernel, out_shape=(jax.ShapeDtypeStruct((rows, 128), BF),...]
    unnamed x4 -> x3, local copies, waits for them, and re-layouts: 3.69 us -> 0.61 us
    pallas_call x0 -> x1, Pallas kernels: none -> 2.4 us  [per_device(): pl.pallas_call(hand_over, out_shape=jax.ShapeDtypeStruct((rows, 128), BF)...]
where the time goes in v4:
time: 57.8 us; the launch traced here: 57.6 us
  Pallas kernels  56.3 us (97%)
  between operations  0.66 us (1%)
  local copies, waits for them, and re-layouts  0.61 us (1%)
    pallas_call x1, Pallas kernels, per_device(): pl.pallas_call(kernel, out_shape=(jax.ShapeDtypeStruct((rows, 128), BF),...  53.9 us
    pallas_call x1, Pallas kernels, per_device(): pl.pallas_call(hand_over, out_shape=jax.ShapeDtypeStruct((rows, 128), BF)...  2.4 us

profile of v4, /device:TPU:11, one launch (start us, length us, event | category | flops | bytes accessed | tf_op | source)
XLA Modules:
  0.0 57.6 jit_solution(12778905714296888386)
XLA Ops:
  0.6 53.9 %shard_map.77 = (bf16[8192,128]{1,0:T(8,128)(2,1)}, f32[16,32]{1,0:T(8,128)}) custom-call(bf16[8192,128]{1,0:T(8,128)(2,1)} %bitcast.8, bf16[8192,128]{1,0:T(8,128)(2,1)} %bitcast.9, f32[64,128]{1,0:T(8,128)} %bitcast.10, bf16[256,16384]{1,0:T(8,128)(2,1)} %sb_hbm.1, s32[1,1024]{1,0:T(1,128)} %bitcast.12, s32[4]{0:T(128)} %bitcast.13), custom_call_target="tpu_custom_call" | custom-call | tf_op jit(solution)/shard_map/pallas_call | solution.py:510
  54.6 0.0 copy-start
  54.6 2.4 %shard_map.78 = bf16[8192,128]{1,0:T(8,128)(2,1)} custom-call(bf16[8192,128]{1,0:T(8,128)(2,1)} %get-tuple-element.4.src), custom_call_target="tpu_custom_call" | custom-call | tf_op jit(solution)/shard_map/pallas_call | solution.py:527
  57.0 0.0 copy-done
  57.0 0.6 %copy.9 = f32[32,16]{0,1:T(8,128)} copy(f32[32,16]{0,1:T(8,128)S(1)} %bitcast.11) | data formatting | bytes 4096
Async XLA Ops:
  54.6 2.4 %copy-start = (f32[16,32]{1,0:T(8,128)S(1)}, f32[16,32]{1,0:T(8,128)}, u32[]{:S(2)}) copy-start(f32[16,32]{1,0:T(8,128)} %get-tuple-element.5) | copy-start | bytes 6148

commit v5 on v4

--- a/solution.py
+++ b/solution.py
@@ -37,14 +37,14 @@
 
 
 def kernel(
-    field_hbm, load_hbm, coef_ref, sb_hbm, tcell_ref, fcell_ref,
+    field_hbm, load_hbm, coef_hbm, sb_hbm, tcell_hbm, fcell_hbm,
     out_hbm, flux_ref,
     v0, ld, v1, v2, v3, sb, tr, w4, hb, fs, zh, zs,
     ah, emat, ss, gg, wz, uu, m4, picked, cbuf, c2, pbuf, xall,
     part, cown, csend, crecv, qbuf, zrecv, fbuf, fall,
     gbuf, gnb, cinfo, cnb, lmask, zcols, zcols3, val, val3,
     insem, ldsem, sbsem, outsem, hs_s, hs_r, ts_s, ts_r, c_s, c_r, z_s, z_r, round_sem,
-    f_s, f_r, g_s, g_r, i_s, i_r,
+    f_s, f_r, g_s, g_r, i_s, i_r, tcell_ref, coef_ref, fcell_ref, small,
 ):
     r = lax.axis_index("row")
     c = lax.axis_index("col")
@@ -62,6 +62,26 @@
             src_ref=src, dst_ref=dst, send_sem=ss, recv_sem=rs, device_id=dev, device_id_type=MESH
         )
 
+    count = sum(jnp.where(e, 1, 0) for e in exists)
+
+    def beside(ref, ss, rs, receive):
+        for n in range(3, 7):
+            @pl.when(count == n)
+            def _(n=n):
+                some = ref.at[pl.ds(0, n)]
+                cp = rcopy(some, some, ss, rs, {"row": right})
+                if receive:
+                    cp.wait_recv()
+                else:
+                    cp.wait_send()
+
+    smalls = [
+        pltpu.make_async_copy(tcell_hbm, tcell_ref, small.at[0]),
+        pltpu.make_async_copy(coef_hbm, coef_ref, small.at[1]),
+        pltpu.make_async_copy(fcell_hbm, fcell_ref, small.at[2]),
+    ]
+    for cp in smalls:
+        cp.start()
     barrier = pltpu.get_barrier_semaphore()
 
     def greet(dev):
@@ -95,6 +115,7 @@
         cp.start()
         cin.append(cp)
 
+    smalls[0].wait()
     cell = tcell_ref[...]
     chosen_xy = onehot((cell >> 7) == iota((64, 1024), 0))
     chosen_z = onehot((cell & 127) == iota((128, 1024), 0))
@@ -204,6 +225,7 @@
                 arrived(base + 1, 1)
 
     def faces(s, i, pairs):
+        edge = ([], [])
         for n, pair in enumerate(pairs):
             f = mm(emat[...], pair).astype(BF)
             for j in range(2):
@@ -213,17 +235,22 @@
             v = jnp.concatenate([pair[:, :128], pair[:, 128:]], axis=0)
             zf = nt(wz[...], v)
             for d in range(2):
-                zs[s, d, i, n:n + 1, :] = zf[d:d + 1, :]
+                edge[d].extend([zf[d:d + 1, :128], zf[d:d + 1, 128:]])
+        for d in range(2):
+            zs[s, d, i] = jnp.concatenate(edge[d], axis=0).astype(BF)
 
     def sweep(s, i, vin, vout, more_rows, cols):
         v = [vin[pl.ds(pl.multiple_of(i * 1024 + n * 128, 128), 128), :] for n in range(8)]
         rid = iota((16, 256), 0)
+        edge = [zh[s, d, i].astype(F32) for d in range(2)]
         lhs = []
         for n in range(2):
             ends = jnp.zeros((16, 256), F32)
             for j in range(2):
                 for d in range(2):
-                    ends = jnp.where(rid == 2 * j + d, zh[s, d, i, 2 * n + j:2 * n + j + 1, :], ends)
+                    at = 4 * n + 2 * j
+                    row = jnp.concatenate([edge[d][at:at + 1, :], edge[d][at + 1:at + 2, :]], axis=1)
+                    ends = jnp.where(rid == 2 * j + d, row, ends)
             lhs.append(ends)
         lhs = jnp.concatenate([jnp.concatenate(lhs, axis=1)] + more_rows, axis=0).astype(BF)
         t = tn(lhs, cols)
@@ -287,6 +314,8 @@
     p, q = iota((16, 256), 0), iota((16, 256), 1)
     uu[...] = jnp.where(p < 4, jnp.where(q == (p >> 1) * 128 + (p & 1) * 127, 1.0, 0.0), 0.0).astype(BF)
 
+    smalls[1].wait()
+    smalls[2].wait()
     w = OMEGA / (6.0 + coef_ref[...])
     for k in range(2):
         w4[k * 64:(k + 1) * 64, :] = w
@@ -304,7 +333,7 @@
     for d in range(6):
         @pl.when(exists[d])
         def _(d=d):
-            rcopy(cinfo, cnb.at[d ^ 1], i_s.at[d], i_r.at[d ^ 1], nbid[d]).start()
+            rcopy(cinfo, cnb.at[d ^ 1], i_s, i_r, nbid[d]).start()
 
     for d in range(6):
         @pl.when(jnp.logical_not(exists[d]))
@@ -317,7 +346,7 @@
                     def _(k, s=s):
                         hb[s, d, pl.ds(pl.multiple_of(k * 128, 128), 128), :] = jnp.zeros((128, 128), BF)
                 else:
-                    zh[s, d - 4] = jnp.zeros((GROUPS, 4, 256), F32)
+                    zh[s, d - 4] = jnp.zeros((GROUPS, 8, 128), BF)
 
     @pl.loop(0, 8)
     def _(k):
@@ -365,10 +394,7 @@
         rcopy(qbuf.at[j], zrecv.at[me], z_s, z_r, holder(j)).start()
     sweep1(1, 4)
 
-    for d in range(6):
-        @pl.when(exists[d])
-        def _(d=d):
-            rcopy(cnb.at[d], cnb.at[d], i_s.at[d], i_r.at[d], nbid[d]).wait_recv()
+    beside(cnb, i_s, i_r, True)
     mine = iota((8, 128), 0) < 4
     lane = iota((8, 256), 1) & 63
     for k in range(7):
@@ -409,17 +435,14 @@
     for d in range(6):
         @pl.when(exists[d])
         def _(d=d):
-            rcopy(gbuf, gnb.at[d ^ 1], g_s.at[d], g_r.at[d ^ 1], nbid[d]).start()
+            rcopy(gbuf, gnb.at[d ^ 1], g_s, g_r, nbid[d]).start()
     fall[g] = own
     for o in range(1, 4):
         cp = rcopy(fbuf, fall.at[g], f_s, f_r, {"gz": (g + o) % 4})
         cp.start()
     sweep1(4, 8)
 
-    for d in range(6):
-        @pl.when(exists[d])
-        def _(d=d):
-            rcopy(gnb.at[d], gnb.at[d], g_s.at[d], g_r.at[d], nbid[d]).wait_recv()
+    beside(gnb, g_s, g_r, True)
 
     def split(values):
         hi = values.astype(BF).astype(F32)
@@ -439,6 +462,13 @@
         faces(2, k, sweep(1, k, v1, v2, rows, zcols[...].astype(BF)))
         send_halos(2, k)
 
+    others = pl.ds(0, 3)
+    fgot = rcopy(qbuf.at[others], fall.at[others], f_s, f_r, {"gz": (g + 1) % 4})
+    fgot.wait_recv()
+    sel = jnp.where(iota((32, 128), 1) == g * 32 + iota((32, 128), 0), 1.0, 0.0)
+    rows16 = jnp.concatenate([fall[0], fall[1], fall[2], fall[3]], axis=0)
+    flux_ref[...] = nt(rows16, sel, precision=lax.Precision.HIGHEST)
+
     def put(k):
         rows = pl.ds(pl.multiple_of(k * 1024, 1024), 1024)
         return pltpu.make_async_copy(v3.at[rows], out_hbm.at[rows], outsem)
@@ -450,13 +480,8 @@
         sweep(2, k, v2, v3, rows, zcols3[...].astype(BF))
         put(k).start()
 
-    others = pl.ds(0, 3)
-    fgot = rcopy(qbuf.at[others], fall.at[others], f_s, f_r, {"gz": (g + 1) % 4})
-    fgot.wait_recv()
-    sel = jnp.where(iota((32, 128), 1) == g * 32 + iota((32, 128), 0), 1.0, 0.0)
-    rows16 = jnp.concatenate([fall[0], fall[1], fall[2], fall[3]], axis=0)
-    flux_ref[...] = nt(rows16, sel, precision=lax.Precision.HIGHEST)
-
+    beside(cnb, i_s, i_r, False)
+    beside(gnb, g_s, g_r, False)
     sent = pl.ds(0, 3)
     rcopy(tr.at[sent], tr.at[sent], ts_s, ts_r.at[0], {"row": right}).wait_send()
     for cp in (core, zall, fgot):
@@ -464,23 +489,25 @@
     for d in range(6):
         @pl.when(exists[d])
         def _(d=d):
-            rcopy(cinfo, cnb.at[d ^ 1], i_s.at[d], i_r.at[d ^ 1], nbid[d]).wait_send()
-            rcopy(gbuf, gnb.at[d ^ 1], g_s.at[d], g_r.at[d ^ 1], nbid[d]).wait_send()
             sent = fs.at[:, d] if d < 4 else zs.at[:, d - 4]
             rcopy(sent, sent, hs_s.at[d], hs_r.at[0, d // 2, 0], nbid[d]).wait_send()
     pltpu.make_async_copy(v3, out_hbm, outsem).wait()
 
 
-def hand_over(src, dst, held, came, left):
+def hand_over(src, flux, dst, flux_out, held, small, came, left, sides):
     into = [pltpu.make_async_copy(src.at[pl.ds(k * 1024, 1024)], held.at[k], came.at[k]) for k in range(8)]
-    out = [pltpu.make_async_copy(held.at[k], dst.at[pl.ds(k * 1024, 1024)], left.at[k]) for k in range(8)]
     for cp in into:
         cp.start()
+    first = pltpu.make_async_copy(flux, small, sides.at[0])
+    second = pltpu.make_async_copy(small, flux_out, sides.at[1])
+    first.start()
     for k in range(8):
         into[k].wait()
-        out[k].start()
-    for cp in out:
-        cp.wait()
+        pltpu.make_async_copy(held.at[k], dst.at[pl.ds(k * 1024, 1024)], left).start()
+    first.wait()
+    second.start()
+    pltpu.make_async_copy(src, dst, left).wait()
+    second.wait()
 
 
 def per_device(volume_field, volume_load, coefficient, surface_block, trace_cell, flux_cell):
@@ -491,7 +518,7 @@
     scratch = [
         vm((rows, 128), BF), vm((rows, 128), BF), vm((rows, 128), BF), vm((rows, 128), BF), vm((rows, 128), BF),
         vm((4, 256, 1024), BF), vm((4, 2, 128, 512), BF), vm((128, 128), F32),
-        vm((3, 4, 1024, 128), BF), vm((3, 4, 1024, 128), BF), vm((3, 2, GROUPS, 4, 256), F32), vm((3, 2, GROUPS, 4, 256), F32),
+        vm((3, 4, 1024, 128), BF), vm((3, 4, 1024, 128), BF), vm((3, 2, GROUPS, 8, 128), BF), vm((3, 2, GROUPS, 8, 128), BF),
         vm((128, 192), BF), vm((64, 128), BF), vm((256, 256), BF), vm((1024, 128), BF),
         vm((16, 128), BF), vm((16, 256), BF), vm((256, 128), BF), vm((rows, 128), F32),
         vm((1024, 128), F32), vm((128, 1024), BF),
@@ -502,7 +529,8 @@
         vm((8, 128), F32), vm((6, 8, 128), F32), vm((8, 128), F32), vm((6, 8, 128), F32),
         vm((56, 256), F32), vm((128, 256), F32), vm((32, 256), F32), vm((56, 128), F32), vm((8, 128), F32),
         dma((4,)), dma, dma, dma, dma((6,)), dma((2, 3, GROUPS)),
-        dma, dma((4,)), dma, dma, dma, dma, pltpu.SemaphoreType.REGULAR, dma, dma, dma((6,)), dma((6,)), dma((6,)), dma((6,)),
+        dma, dma((4,)), dma, dma, dma, dma, pltpu.SemaphoreType.REGULAR, dma, dma, dma, dma, dma, dma,
+        vm((1, 1024), I32), vm((64, 128), F32), pltpu.SMEM((4,), I32), dma((3,)),
     ]
     anywhere = pl.BlockSpec(memory_space=pl.ANY)
     outside = pl.BlockSpec(memory_space=pltpu.HBM)
@@ -510,7 +538,7 @@
     new_field, surface_flux = pl.pallas_call(
         kernel,
         out_shape=(jax.ShapeDtypeStruct((rows, 128), BF), jax.ShapeDtypeStruct((16, 32), F32)),
-        in_specs=[outside, outside, local, outside, local, pl.BlockSpec(memory_space=pltpu.SMEM)],
+        in_specs=[anywhere] * 6,
         out_specs=(anywhere, local),
         scratch_shapes=scratch,
         compiler_params=pltpu.CompilerParams(
@@ -524,13 +552,13 @@
         trace_cell.reshape(1, 1024),
         flux_cell.reshape(4),
     )
-    new_field = pl.pallas_call(
+    new_field, surface_flux = pl.pallas_call(
         hand_over,
-        out_shape=jax.ShapeDtypeStruct((rows, 128), BF),
-        in_specs=[anywhere],
-        out_specs=anywhere,
-        scratch_shapes=[vm((8, rows // 8, 128), BF), dma((8,)), dma((8,))],
-    )(new_field)
+        out_shape=(jax.ShapeDtypeStruct((rows, 128), BF), jax.ShapeDtypeStruct((16, 32), F32)),
+        in_specs=[anywhere, anywhere],
+        out_specs=(anywhere, anywhere),
+        scratch_shapes=[vm((8, rows // 8, 128), BF), vm((16, 32), F32), dma((8,)), dma, dma((2,))],
+    )(new_field, surface_flux)
     return new_field.reshape(volume_field.shape), surface_flux.T
 
 

time: 57.8 us -> 55.5 us (0.960)
  Pallas kernels: 56.3 us -> 54.7 us
  local copies, waits for them, and re-layouts: 0.61 us -> 0 us
    pallas_call x1, Pallas kernels: 53.9 us -> 52.3 us  [per_device(): pl.pallas_call(kernel, out_shape=(jax.ShapeDtypeStruct((rows, 128), BF),...]
    unnamed x3 -> x0, local copies, waits for them, and re-layouts: 0.61 us -> none
where the time goes in v5:
time: 55.5 us; the launch traced here: 55.3 us
  Pallas kernels  54.7 us (99%)
  between operations  0.64 us (1%)
    pallas_call x1, Pallas kernels, per_device(): pl.pallas_call(kernel, out_shape=(jax.ShapeDtypeStruct((rows, 128), BF),...  52.3 us
    pallas_call x1, Pallas kernels, per_device(): pl.pallas_call(hand_over, out_shape=(jax.ShapeDtypeStruct((rows, 128), BF...  2.35 us

profile of v5, /device:TPU:11, one launch (start us, length us, event | category | flops | bytes accessed | tf_op | source)
XLA Modules:
  0.0 55.3 jit_solution(5037709828005830743)
XLA Ops:
  0.6 52.3 %shard_map.77 = (bf16[8192,128]{1,0:T(8,128)(2,1)}, f32[16,32]{1,0:T(8,128)}) custom-call(bf16[8192,128]{1,0:T(8,128)(2,1)} %bitcast.7, bf16[8192,128]{1,0:T(8,128)(2,1)} %bitcast.8, f32[64,128]{1,0:T(8,128)} %bitcast.9, bf16[256,16384]{1,0:T(8,128)(2,1)} %sb_hbm.1, s32[1,1024]{1,0:T(1,128)} %bitcast.10, s32[4]{0:T(128)} %bitcast.11), custom_call_target="tpu_custom_call" | custom-call | tf_op jit(solution)/shard_map/pallas_call | solution.py:538
  53.0 2.4 %shard_map.78 = (bf16[8192,128]{1,0:T(8,128)(2,1)}, f32[16,32]{1,0:T(8,128)}) custom-call(bf16[8192,128]{1,0:T(8,128)(2,1)} %get-tuple-element.6.src, f32[16,32]{1,0:T(8,128)} %get-tuple-element.7.flux), custom_call_target="tpu_custom_call" | custom-call | tf_op jit(solution)/shard_map/pallas_call | solution.py:555
